TPU v7x, 32 devices: a whole 2x2x4 slice. The times are simulated.
32 devices in a mesh: px: 16 (over z, y, core), py: 2 (over x).
Axes of the slice: x: 2, y: 2, z: 4, core: 2. Of those that a mesh axis runs over, the one named last changes fastest.
Arguments:
- spectrum: float32 [2, 3, 128, 128, 512], P(None, None, 'px', 'py'), may hold values from -3 to 3
- scalar: float32 [1024, 256, 256], P('px', 'py'), may hold values from -6 to 6
Outputs:
- tendency: float32 [2, 3, 128, 128, 512], P(None, None, 'px', 'py')
- advanced: float32 [1024, 256, 256], P('px', 'py')
All inputs are finite; a program needn't handle non-finite values.
Results may differ from a plain program's by a relative error of at most 0.0003.
Values sent between devices are 32-bit elements; how exact they have to be, the bound alone decides.
A program may use at most 320 MiB of HBM per device.

v0:
```python
import math

import jax
import jax.numpy as jnp
from jax import lax
from jax.sharding import PartitionSpec as P

NSUB = 3


STEP_RATIO = 0.08
DIFFUSION_RATIO = 1.0


def padded(block, sides, width):
    for axis, dim in sides:
        count = lax.axis_size(axis)
        forward = [(i, i + 1) for i in range(count - 1)]
        forward.append((count - 1, 0))
        backward = [(target, source) for source, target in forward]
        low = lax.ppermute(
            lax.slice_in_dim(block, block.shape[dim] - width, None, axis=dim), axis, forward
        )
        high = lax.ppermute(lax.slice_in_dim(block, 0, width, axis=dim), axis, backward)
        block = jnp.concatenate([low, block, high], axis=dim)
    return block


def contract(form, left, right):
    return jnp.einsum(form, left, right, precision=lax.Precision.HIGHEST)


def dft_table(length, sign):
    index = jnp.arange(length, dtype=jnp.int32)
    product = index[:, None] * index[None, :] % length
    angle = 2.0 * math.pi / length * product.astype(jnp.float32)
    return (jnp.cos(angle), sign * jnp.sin(angle))


def complex_apply(real, imag, cosine, sine, form):
    return (
        contract(form, real, cosine) - contract(form, imag, sine),
        contract(form, real, sine) + contract(form, imag, cosine),
    )


def upsample_table(length):
    rows = jnp.arange(length, dtype=jnp.int32)[:, None]
    cols = jnp.arange(2 * length, dtype=jnp.int32)[None, :]
    half = cols // 2
    is_odd = cols % 2 == 1
    near = jnp.logical_or(rows == half, rows == (half + 1) % length)
    distant = jnp.logical_or(rows == (half - 1) % length, rows == (half + 2) % length)
    even_part = jnp.where(jnp.logical_and(jnp.logical_not(is_odd), rows == half), 1.0, 0.0)
    odd_part = jnp.where(
        is_odd, jnp.where(near, 9.0 / 16.0, 0.0) - jnp.where(distant, 1.0 / 16.0, 0.0), 0.0
    )
    return (even_part + odd_part).astype(jnp.float32)


def pair_table(length):
    rows = jnp.arange(2 * length, dtype=jnp.int32)[:, None]
    cols = jnp.arange(length, dtype=jnp.int32)[None, :]
    return jnp.where(rows // 2 == cols, 0.125, 0.0).astype(jnp.float32)


def wavenumbers(length):
    index = jnp.arange(length, dtype=jnp.int32)
    signed = jnp.where(index < length // 2, index, index - length)
    return 2.0 * math.pi / length * signed.astype(jnp.float32)


def across_px(pieces):
    return lax.all_to_all(pieces, "px", split_axis=2, concat_axis=1, tiled=True)


def across_py(pieces):
    return lax.all_to_all(pieces, "py", split_axis=2, concat_axis=1, tiled=True)


def slab(array, start, stop, axis):
    return lax.slice_in_dim(array, start, stop, axis=axis)


def refine(field, axis):
    count = field.shape[axis]
    points = slab(field, 2, count - 1, axis)
    middles = (
        9.0 * (slab(field, 1, count - 2, axis) + points)
        - (slab(field, 0, count - 3, axis) + slab(field, 3, count, axis))
    ) / 16.0
    paired = jnp.concatenate([middles, points], axis=axis + 1)
    shape = list(field.shape)
    shape[axis] = 2 * (count - 3)
    return paired.reshape(shape)


def limited_slope(first, second):
    return 0.5 * (jnp.sign(first) + jnp.sign(second)) * jnp.minimum(jnp.abs(first), jnp.abs(second))


def spin_divergence(theta, speed, axis):
    ahead = jnp.roll(theta, -1, axis)
    jump = ahead - theta
    slope = limited_slope(jnp.roll(jump, 1, axis), jump)
    left = theta + 0.5 * slope
    right = ahead - 0.5 * jnp.roll(slope, -1, axis)
    face = 0.5 * (speed + jnp.roll(speed, -1, axis))
    flux = jnp.maximum(face, 0.0) * left + jnp.minimum(face, 0.0) * right - DIFFUSION_RATIO * jump
    return flux - jnp.roll(flux, 1, axis)


def divergence(theta, speed, axis):
    count = theta.shape[axis]
    jump = slab(theta, 1, count, axis) - slab(theta, 0, count - 1, axis)
    slope = limited_slope(slab(jump, 0, count - 2, axis), slab(jump, 1, count - 1, axis))
    left = slab(theta, 1, count - 2, axis) + 0.5 * slab(slope, 0, count - 3, axis)
    right = slab(theta, 2, count - 1, axis) - 0.5 * slab(slope, 1, count - 2, axis)
    face = 0.5 * (slab(speed, 0, count - 3, axis) + slab(speed, 1, count - 2, axis))
    flux = (
        jnp.maximum(face, 0.0) * left
        + jnp.minimum(face, 0.0) * right
        - DIFFUSION_RATIO * slab(jump, 1, count - 2, axis)
    )
    return slab(flux, 1, count - 3, axis) - slab(flux, 0, count - 4, axis)


def advance(theta, speed):
    flow_first = divergence(theta[:, 1:-1], speed[0], 0)[:, 1:-1]
    flow_second = divergence(theta[1:-1, :], speed[1], 1)[1:-1, :]
    flow_third = spin_divergence(theta[1:-1, 1:-1], speed[2], 2)[1:-1, 1:-1]
    return theta[2:-2, 2:-2] - STEP_RATIO * (flow_first + flow_second + flow_third)


def body(spectrum, scalar):
    groups_x = lax.axis_size("px")
    groups_y = lax.axis_size("py")
    spec_second = spectrum.shape[2]
    spec_third = spectrum.shape[3]
    length_first = spectrum.shape[4]
    length_second = spec_second * groups_x
    length_third = spec_third * groups_y
    cells_first = length_first // groups_x
    cells_second = length_second // groups_y
    factor = 1.0 / math.sqrt(length_first * length_second * length_third)
    wave_first = wavenumbers(length_first)
    third_local = lax.dynamic_slice_in_dim(
        wavenumbers(length_third), lax.axis_index("py") * spec_third, spec_third
    )
    real_part = spectrum[0]
    imag_part = spectrum[1]
    first_cos, first_sin = dft_table(length_first, 1.0)
    line_wave = wave_first[None, None, None, :]
    real_fields = jnp.concatenate([real_part, -line_wave * imag_part[1:]])
    imag_fields = jnp.concatenate([imag_part, line_wave * real_part[1:]])
    real_lines = jnp.transpose(real_fields, (1, 0, 2, 3)).reshape(
        spec_second, 5 * spec_third, length_first
    )
    imag_lines = jnp.transpose(imag_fields, (1, 0, 2, 3)).reshape(
        spec_second, 5 * spec_third, length_first
    )
    out_real, out_imag = complex_apply(real_lines, imag_lines, first_cos, first_sin, "qlk,kx->qxl")
    landed = across_px(jnp.stack([out_real, out_imag]))
    wave_second = wavenumbers(length_second)[:, None, None]
    wave_third = third_local[None, None, :]
    real_in = landed[0]
    imag_in = landed[1]

    def member(array, index):
        return array[..., index * spec_third : (index + 1) * spec_third]

    omega_real = [
        -(wave_second * member(imag_in, 2) - wave_third * member(imag_in, 1)),
        -wave_third * member(imag_in, 0) - member(real_in, 4),
        member(real_in, 3) + wave_second * member(imag_in, 0),
    ]
    omega_imag = [
        wave_second * member(real_in, 2) - wave_third * member(real_in, 1),
        wave_third * member(real_in, 0) - member(imag_in, 4),
        member(imag_in, 3) - wave_second * member(real_in, 0),
    ]
    arrived = jnp.stack(
        [
            jnp.concatenate([real_in[..., : 3 * spec_third]] + omega_real, axis=-1),
            jnp.concatenate([imag_in[..., : 3 * spec_third]] + omega_imag, axis=-1),
        ]
    )
    second_cos, second_sin = dft_table(length_second, 1.0)
    out_real, out_imag = complex_apply(
        arrived[0], arrived[1], second_cos, second_sin, "pxl,py->yxl"
    )
    arrived = across_py(jnp.stack([out_real, out_imag])[:, None])
    ordered = arrived.reshape(2, groups_y, cells_second, cells_first, 6, spec_third)
    ordered = jnp.transpose(ordered, (0, 4, 3, 2, 1, 5)).reshape(
        2, 6, cells_first, cells_second, length_third
    )
    third_cos, third_sin = dft_table(length_third, 1.0)
    physical = (
        contract("cxyn,nz->cxyz", ordered[0], third_cos)
        - contract("cxyn,nz->cxyz", ordered[1], third_sin)
    ) * factor
    velocity = physical[:3]
    vorticity = physical[3:]
    widened = padded(velocity, (("px", 1), ("py", 2)), 4)
    speed = contract("cxyz,zw->cxyw", widened, upsample_table(length_third))
    speed = refine(speed, 1)
    speed = refine(speed, 2)
    theta = scalar
    inner_speed = speed[:, 4:-4, 4:-4]
    for turn in range(NSUB):
        grown = padded(theta, (("px", 0), ("py", 1)), 2)
        theta = advance(grown, inner_speed)
    pair_first = theta.reshape(cells_first, 2, 2 * cells_second, 2 * length_third).sum(axis=1)
    pair_both = pair_first.reshape(cells_first, cells_second, 4 * length_third)
    pair_both = pair_both[..., : 2 * length_third] + pair_both[..., 2 * length_third :]
    buoyancy = contract("xyw,wz->xyz", pair_both, pair_table(length_third))
    forcing = jnp.stack(
        [
            velocity[1] * vorticity[2] - velocity[2] * vorticity[1],
            velocity[2] * vorticity[0] - velocity[0] * vorticity[2],
            velocity[0] * vorticity[1] - velocity[1] * vorticity[0] + buoyancy,
        ]
    )
    back_cos, back_sin = dft_table(length_third, -1.0)
    force_lines = forcing.reshape(3 * cells_first * cells_second, length_third)
    sectioned = jnp.stack(
        [contract("lz,zn->nl", force_lines, back_cos), contract("lz,zn->nl", force_lines, back_sin)]
    )
    arrived = across_py(sectioned[:, None])
    ordered = arrived.reshape(2, groups_y, spec_third, 3, cells_first, cells_second)
    ordered = jnp.transpose(ordered, (0, 2, 3, 4, 1, 5)).reshape(
        2, spec_third * 3 * cells_first, length_second
    )
    back_cos, back_sin = dft_table(length_second, -1.0)
    out_real, out_imag = complex_apply(ordered[0], ordered[1], back_cos, back_sin, "ly,yp->pl")
    arrived = across_px(jnp.stack([out_real, out_imag])[:, None])
    ordered = arrived.reshape(2, groups_x, spec_second, spec_third, 3, cells_first)
    ordered = jnp.transpose(ordered, (0, 4, 2, 3, 1, 5)).reshape(
        2, 3, spec_second, spec_third, length_first
    )
    back_cos, back_sin = dft_table(length_first, -1.0)
    out_real, out_imag = complex_apply(ordered[0], ordered[1], back_cos, back_sin, "cqsx,xk->cqsk")
    tendency = jnp.stack([out_real, out_imag]) * factor
    return (tendency, theta)


def solution(mesh):
    in_specs = (P(None, None, "px", "py", None), P("px", "py", None))
    out_specs = (P(None, None, "px", "py", None), P("px", "py", None))
    return jax.shard_map(body, mesh=mesh, in_specs=in_specs, out_specs=out_specs, check_vma=False)
```

profile of v0, /device:TPU:1, one launch (start us, length us, event | category | flops | bytes accessed | tf_op | source)
XLA Modules:
  0.0 2149.3 jit_solution(10865645601107310046)
XLA Ops:
  84.6 224.1 %all-to-all-done = f32[2,8,512,320]{3,1,0,2:T(8,128)} async-done(((f32[2,8,512,320]{3,1,0,2:T(8,128)}), f32[2,8,512,320]{3,1,0,2:T(8,128)}, u32[]{:S(2)}, u32[]{:S(2)}) %all-to-all-start) | async-done | bytes 10485792 | tf_op jit(solution)/shard_map/all_to_all | solution.py:74
  422.3 16.6 collective-permute-start.4
  450.8 111.3 %collective-permute-done.7 = f32[68,2,256]{2,0,1:T(8,128)S(1)} collective-permute-done((f32[68,2,256]{2,0,1:T(8,128)S(1)}, f32[68,2,256]{2,0,1:T(8,128)S(1)}, u32[]{:S(2)}, u32[]{:S(2)}) %collective-permute-start.7) | collective-permute-done | bytes 139296 | tf_op jit(solution)/shard_map/ppermute | solution.py:24
  601.7 16.5 minimum_multiply_fusion.7
  646.9 24.7 %reshape.262 = f32[2,2,64,32,6,64]{2,1,5,4,3,0:T(2,128)} reshape(f32[2,1,128,32,384]{2,4,3,0,1:T(8,128)} %copy.75) | data formatting | bytes 25165824 | tf_op jit(solution)/shard_map/reshape | solution.py:193
  671.5 25.1 %fusion.290 = (f32[1,6,32,64,2,64]{3,4,5,1,2,0:T(2,128)}, f32[1,6,32,64,2,64]{3,4,5,1,2,0:T(2,128)}) fusion(f32[2,6,32,64,2,64]{3,4,5,1,2,0:T(2,128)} %bitcast.177), kind=kLoop, calls=%fused_computation.429 | loop fusion | bytes 25165824 | tf_op jit(solution)/shard_map/slice | solution.py:200
  696.7 22.8 %copy.76 = f32[1,6,32,64,2,64]{5,4,3,2,1,0:T(2,128)} copy(f32[1,6,32,64,2,64]{3,4,5,1,2,0:T(2,128)} %get-tuple-element.15) | data formatting | bytes 12582912 | tf_op jit(solution)/shard_map/slice | solution.py:199
  741.5 22.8 %copy.77 = f32[1,6,32,64,2,64]{5,4,3,2,1,0:T(2,128)} copy(f32[1,6,32,64,2,64]{3,4,5,1,2,0:T(2,128)} %get-tuple-element.14) | data formatting | bytes 12582912 | tf_op jit(solution)/shard_map/slice | solution.py:200
  790.6 17.2 collective-permute-start
  822.2 20.7 collective-permute-done
  907.0 33.8 %fusion.1 = (f32[3,74,69,256]{3,2,1,0:T(8,128)}, f32[3,74,69,256]{3,2,1,0:T(8,128)}) fusion(f32[3,74,72,256]{3,2,1,0:T(8,128)} %bitcast.169), kind=kLoop, calls=%fused_computation.3 | loop fusion | flops 19607040 | bytes 94113792 | tf_op jit(solution)/shard_map/div | solution.py:88
  940.8 25.8 %pad_maximum_fusion = f32[3,74,69,512]{3,2,1,0:T(8,128)} fusion(f32[3,74,69,256]{3,2,1,0:T(8,128)} %get-tuple-element.17, f32[3,74,69,256]{3,2,1,0:T(8,128)} %get-tuple-element.16), kind=kLoop, calls=%fused_computation | loop fusion | flops 7842816 | bytes 62742528 | tf_op jit(solution)/shard_map/concatenate | solution.py:92
  966.6 33.4 %reshape.264 = f32[3,74,138,256]{3,2,1,0:T(8,128)} reshape(f32[3,74,69,512]{3,2,1,0:T(8,128)} %pad_maximum_fusion) | data formatting | bytes 62742528 | tf_op jit(solution)/shard_map/reshape | solution.py:95
  1019.6 31.9 %fusion.23 = (f32[66,130,256]{2,1,0:T(8,128)}, f32[66,130,256]{2,1,0:T(8,128)}) fusion(f32[66,130,256]{2,1,0:T(8,128)} %slice_subtract_fusion.14, f32[66,130,1]{2,1,0:T(8,128)S(1)} %slice-done, f32[66,130,255]{2,1,0:T(8,128)} %slice.848, f32[66,130,256]{2,1,0:T(8,128)} %minimum_multiply_fusion.6, f32[68,132,256]{2,1,0:T(8,128)} %copy-done, ...), kind=kLoop, calls=%fused_computation.69 | loop fusion | flops 32947200 | bytes 79073280 | tf_op jit(solution)/shard_map/sub | solution.py:109
  1057.3 30.6 %slice_subtract_fusion.7 = f32[66,129,256]{2,1,0:T(8,128)} fusion(f32[66,131,256]{2,1,0:T(8,128)} %slice_subtract_fusion.8, f32[66,130,256]{2,1,0:T(8,128)} %minimum_multiply_fusion.7, f32[68,2,256]{2,1,0:T(2,128)S(1)} %copy-done.22, f32[68,128,256]{2,1,0:T(8,128)} %copy-done.11, f32[68,2,256]{2,1,0:T(2,128)S(1)} %copy-done.24, ...), kind=kLoop, calls=%fused_computation.47 | loop fusion | flops 30514176 | bytes 61501440 | tf_op jit(solution)/shard_map/sub | solution.py:121
  1099.1 25.9 %slice_subtract_fusion.11 = f32[65,130,256]{2,1,0:T(8,128)} fusion(f32[67,130,256]{2,1,0:T(8,128)} %slice_subtract_fusion.2, f32[66,130,256]{2,1,0:T(8,128)} %minimum_multiply_fusion.8, f32[68,132,256]{2,1,0:T(8,128)} %copy-done, f32[3,74,138,256]{3,2,1,0:T(8,128)} %reshape.264), kind=kLoop, calls=%fused_computation.109 | loop fusion | flops 25958400 | bytes 69222400 | tf_op jit(solution)/shard_map/sub | solution.py:121
  1137.0 24.4 %fusion.58 = f32[64,128,256]{2,1,0:T(8,128)S(1)} fusion(f32[64,128,256]{2,1,0:T(8,128)} %param.3, f32[66,130,256]{2,1,0:T(8,128)} %get-tuple-element.6, f32[66,130,255]{2,1,0:T(8,128)} %bitcast.175, f32[66,130,1]{2,1,0:T(8,128)} %slice.850, f32[66,128,256]{2,1,0:T(8,128)} %get-tuple-element.33, f32[66,128,256]{2,1,0:T(8,128)} %get-tuple-element.32, ...), kind=kLoop, calls=%fused_computation.141 | loop fusion | flops 16777216 | bytes 67506176 | tf_op jit(solution)/shard_map/sub | solution.py:132
  1247.7 25.4 %fusion.27 = f32[66,130,256]{2,1,0:T(8,128)} fusion(f32[66,130,256]{2,1,0:T(8,128)} %copy-done.5, f32[66,130,1]{2,1,0:T(8,128)} %slice.885, f32[66,130,255]{2,1,0:T(8,128)} %slice.884, f32[66,130,256]{2,1,0:T(8,128)} %copy-done.7, f32[68,132,256]{2,1,0:T(8,128)} %copy-done.2, f32[66,130,256]{2,1,0:T(8,128)} %get-tuple-element.7, f32[66,130,1]{2,1,0:T(8,128)} %slice.881, ...), kind=kLoop, calls=%fused_computation.76 | loop fusion | flops 26357760 | bytes 61501440 | tf_op jit(solution)/shard_map/sub | solution.py:109
  1295.0 22.4 %slice_subtract_fusion.5 = f32[66,129,256]{2,1,0:T(8,128)S(1)} fusion(f32[66,131,256]{2,1,0:T(8,128)} %slice_subtract_fusion.6, f32[66,130,256]{2,1,0:T(8,128)} %minimum_multiply_fusion.4, f32[68,2,256]{2,1,0:T(2,128)S(1)} %copy.87, f32[2,128,256]{2,1,0:T(8,128)S(1)} %collective-permute-done.9, f32[64,128,256]{2,1,0:T(8,128)} %copy-done.4, ...), kind=kLoop, calls=%fused_computation.31 | loop fusion | flops 39232512 | bytes 61501440 | tf_op jit(solution)/shard_map/sub | solution.py:121
  1340.8 25.9 %slice_subtract_fusion.10 = f32[65,130,256]{2,1,0:T(8,128)} fusion(f32[67,130,256]{2,1,0:T(8,128)} %slice_subtract_fusion.1, f32[66,130,256]{2,1,0:T(8,128)} %minimum_multiply_fusion.5, f32[68,132,256]{2,1,0:T(8,128)} %copy-done.2, f32[3,74,138,256]{3,2,1,0:T(8,128)} %reshape.264), kind=kLoop, calls=%fused_computation.101 | loop fusion | flops 25958400 | bytes 69222400 | tf_op jit(solution)/shard_map/sub | solution.py:121
  1378.9 23.8 %fusion.54 = f32[64,128,256]{2,1,0:T(8,128)S(1)} fusion(f32[64,128,256]{2,1,0:T(8,128)} %copy-done.4, f32[66,130,256]{2,1,0:T(8,128)} %fusion.27, f32[66,130,255]{2,1,0:T(8,128)} %bitcast.176, f32[66,130,1]{2,1,0:T(8,128)} %slice.886, f32[66,128,256]{2,1,0:T(8,128)} %get-tuple-element.31, f32[66,128,256]{2,1,0:T(8,128)} %get-tuple-element.30, ...), kind=kLoop, calls=%fused_computation.133 | loop fusion | flops 16777216 | bytes 67506176 | tf_op jit(solution)/shard_map/sub | solution.py:132
  1482.3 25.4 %fusion.31 = f32[66,130,256]{2,1,0:T(8,128)} fusion(f32[66,130,256]{2,1,0:T(8,128)} %copy-done.6, f32[66,130,1]{2,1,0:T(8,128)} %slice.921, f32[66,130,255]{2,1,0:T(8,128)} %slice.920, f32[66,130,256]{2,1,0:T(8,128)} %copy-done.8, f32[68,132,256]{2,1,0:T(8,128)} %copy-done.1, f32[66,130,256]{2,1,0:T(8,128)} %get-tuple-element.7, f32[66,130,1]{2,1,0:T(8,128)} %slice.917, ...), kind=kLoop, calls=%fused_computation.83 | loop fusion | flops 26357760 | bytes 61501440 | tf_op jit(solution)/shard_map/sub | solution.py:109
  1529.6 22.4 %slice_subtract_fusion.3 = f32[66,129,256]{2,1,0:T(8,128)S(1)} fusion(f32[66,131,256]{2,1,0:T(8,128)} %slice_subtract_fusion.4, f32[66,130,256]{2,1,0:T(8,128)} %minimum_multiply_fusion.1, f32[68,2,256]{2,1,0:T(2,128)S(1)} %copy.93, f32[2,128,256]{2,1,0:T(8,128)S(1)} %collective-permute-done.13, f32[64,128,256]{2,1,0:T(8,128)} %copy-done.3, ...), kind=kLoop, calls=%fused_computation.16 | loop fusion | flops 39232512 | bytes 61501440 | tf_op jit(solution)/shard_map/sub | solution.py:121
  1575.3 26.0 %slice_subtract_fusion.9 = f32[65,130,256]{2,1,0:T(8,128)} fusion(f32[67,130,256]{2,1,0:T(8,128)} %slice_subtract_fusion, f32[66,130,256]{2,1,0:T(8,128)} %minimum_multiply_fusion.2, f32[68,132,256]{2,1,0:T(8,128)} %copy-done.1, f32[3,74,138,256]{3,2,1,0:T(8,128)} %reshape.264), kind=kLoop, calls=%fused_computation.93 | loop fusion | flops 25958400 | bytes 69222400 | tf_op jit(solution)/shard_map/sub | solution.py:121
  1611.8 27.7 %bitcast_reduce_fusion = (f32[32,128,256]{2,1,0:T(8,128)}, f32[64,128,256]{2,1,0:T(8,128)}) fusion(f32[64,128,256]{2,1,0:T(8,128)} %copy-done.3, f32[66,130,255]{2,1,0:T(8,128)} %bitcast.174, f32[66,130,1]{2,1,0:T(8,128)} %slice.922, f32[66,130,256]{2,1,0:T(8,128)} %fusion.31, f32[66,128,256]{2,1,0:T(8,128)} %get-tuple-element.29, ...), kind=kLoop, calls=%fused_computation.146 | loop fusion | flops 17825792 | bytes 71700480 | tf_op jit(solution)/shard_map/reduce_sum | solution.py:213
  1665.4 73.2 %all_to_all.42 = f32[2,1,128,6144]{3,0,1,2:T(2,128)} all-to-all(f32[2,1,128,6144]{3,0,1,2:T(2,128)} %copy.96), channel_id=1, replica_groups=mesh['px'=16,'py'=2] {'py'}, dimensions={2} | all-to-all | bytes 12582912 | tf_op jit(solution)/shard_map/all_to_all | solution.py:78
  1751.2 21.1 copy.126
  1818.0 150.1 %all_to_all.43 = f32[2,1,128,6144]{3,0,1,2:T(2,128)S(1)} all-to-all(f32[2,1,128,6144]{3,0,1,2:T(2,128)} %copy.98), channel_id=1, replica_groups=mesh['px'=16,'py'=2] {'px'}, dimensions={2} | all-to-all | bytes 12582912 | tf_op jit(solution)/shard_map/all_to_all | solution.py:74
  1974.5 31.3 %reshape.269 = f32[2,16,8,64,3,32]{5,4,3,2,1,0:T(4,128)} reshape(f32[2,1,128,6144]{3,2,0,1:T(8,128)} %copy.99) | data formatting | bytes 12582912 | tf_op jit(solution)/shard_map/reshape | solution.py:237
  2005.7 25.7 %fusion.289 = (f32[1,3,8,64,16,32]{5,1,3,2,4,0:T(4,128)}, f32[1,3,8,64,16,32]{5,1,3,2,4,0:T(4,128)}) fusion(f32[2,3,8,64,16,32]{5,1,3,2,4,0:T(4,128)} %bitcast.173), kind=kLoop, calls=%fused_computation.428 | loop fusion | bytes 12582912 | tf_op jit(solution)/shard_map/slice | solution.py:242
  2046.3 27.5 %fusion.90 = f32[3,8,64,512]{3,2,1,0:T(8,128)} fusion(f32[3,8,64,512]{2,3,1,0:T(8,128)} %bitcast.178), kind=kOutput, calls=%fused_computation.216 | convolution fusion | flops 4835770368 | bytes 6291456 | tf_op jit(solution)/shard_map/cqsx,xk->cqsk/dot_general | solution.py:30
  2103.1 28.2 %add_bitcast_fusion.2 = f32[1,3,8,64,512]{4,3,2,1,0:T(8,128)S(1)} fusion(f32[3,8,64,512]{3,2,1,0:T(8,128)} %fusion.90, f32[3,8,64,512]{2,3,1,0:T(8,128)} %bitcast.186), kind=kOutput, calls=%fused_computation.183 | convolution fusion | flops 4836294656 | bytes 9437184 | tf_op jit(solution)/shard_map/cqsx,xk->cqsk/dot_general | solution.py:30
  (252 shorter events, 884.0 us)
Async XLA Ops:
  77.1 231.5 %all-to-all-start = ((f32[2,8,512,320]{3,1,0,2:T(8,128)}), f32[2,8,512,320]{3,1,0,2:T(8,128)}, u32[]{:S(2)}, u32[]{:S(2)}) async-start(f32[2,8,512,320]{3,1,0,2:T(8,128)} %copy.66), calls=%async_computation | async-start | bytes 25165824 | tf_op jit(solution)/shard_map/all_to_all | solution.py:74
  412.9 221.2 %all-to-all-start.1 = ((f32[2,1,128,32,384]{4,3,0,1,2:T(8,128)}), f32[2,1,128,32,384]{4,3,0,1,2:T(8,128)}, u32[]{:S(2)}, u32[]{:S(2)}) async-start(f32[2,1,128,32,384]{4,3,0,1,2:T(8,128)} %copy.74), calls=%async_computation.1 | async-start | bytes 25165824 | tf_op jit(solution)/shard_map/all_to_all | solution.py:78
  422.3 19.9 collective-permute-start.4
  439.0 8.7 collective-permute-start.5
  447.7 117.6 %copy-start.11 = (f32[68,128,256]{2,1,0:T(8,128)}, f32[68,128,256]{2,1,0:T(8,128)S(1)}, u32[]{:S(2)}) copy-start(f32[68,128,256]{2,1,0:T(8,128)S(1)} %constant_dynamic-update-slice_fusion) | copy-start | bytes 26738692
  447.8 114.3 %collective-permute-start.7 = (f32[68,2,256]{2,0,1:T(8,128)S(1)}, f32[68,2,256]{2,0,1:T(8,128)S(1)}, u32[]{:S(2)}, u32[]{:S(2)}) collective-permute-start(f32[68,2,256]{2,0,1:T(8,128)S(1)} %copy.79), channel_id=1, source_target_pairs={{1,0},{0,1},{3,2},{2,3},{5,4},{4,5},{7,6},{6,7},{9,8},{8,9},{11,10... | collective-permute-start | bytes 417800 | tf_op jit(solution)/shard_map/ppermute | solution.py:24
  449.6 115.7 %collective-permute-start.6 = (f32[68,2,256]{2,0,1:T(8,128)S(1)}, f32[68,2,256]{2,0,1:T(8,128)S(1)}, u32[]{:S(2)}, u32[]{:S(2)}) collective-permute-start(f32[68,2,256]{2,0,1:T(8,128)S(1)} %copy.78), channel_id=1, source_target_pairs={{0,1},{1,0},{2,3},{3,2},{4,5},{5,4},{6,7},{7,6},{8,9},{9,8},{10,11... | collective-permute-start | bytes 417800 | tf_op jit(solution)/shard_map/ppermute | solution.py:21
  450.8 420.7 %copy-start.29 = (s32[256]{0:T(256)}, s32[256]{0:T(256)S(1)}, u32[]{:S(2)}) copy-start(s32[256]{0:T(256)S(1)} %get-tuple-element.71) | copy-start | bytes 3076
  790.2 32.0 %collective-permute-start.1 = (f32[3,4,64,128]{3,2,1,0:T(8,128)}, f32[3,4,64,128]{3,2,1,0:T(8,128)S(1)}, u32[]{:S(2)}, u32[]{:S(2)}) collective-permute-start(f32[3,4,64,128]{3,2,1,0:T(8,128)} %get-tuple-element.59), channel_id=1, source_target_pairs={{2,0},{4,2},{6,4},{8,6},{10,8},{12,10},{14,12},{16,14},{18,16},{20... | collective-permute-start | bytes 1179656 | tf_op jit(solution)/shard_map/ppermute | solution.py:24
  790.6 52.3 %collective-permute-start = (f32[3,4,64,128]{3,2,1,0:T(8,128)}, f32[3,4,64,128]{3,2,1,0:T(8,128)}, u32[]{:S(2)}, u32[]{:S(2)}) collective-permute-start(f32[3,4,64,128]{3,2,1,0:T(8,128)} %get-tuple-element.58), channel_id=1, source_target_pairs={{0,2},{2,4},{4,6},{6,8},{8,10},{10,12},{12,14},{14,16},{16,18},{18... | collective-permute-start | bytes 1179656 | tf_op jit(solution)/shard_map/ppermute | solution.py:21
  844.6 27.0 %collective-permute-start.3 = (f32[3,40,4,128]{3,2,1,0:T(4,128)}, f32[3,40,4,128]{3,2,1,0:T(4,128)}, u32[]{:S(2)}, u32[]{:S(2)}) collective-permute-start(f32[3,40,4,128]{3,2,1,0:T(4,128)} %get-tuple-element.65), channel_id=1, source_target_pairs={{1,0},{0,1},{3,2},{2,3},{5,4},{4,5},{7,6},{6,7},{9,8},{8,9},{11,10... | collective-permute-start | bytes 737288 | tf_op jit(solution)/shard_map/ppermute | solution.py:24
  844.8 26.7 %collective-permute-start.2 = (f32[3,40,4,128]{3,2,1,0:T(4,128)}, f32[3,40,4,128]{3,2,1,0:T(4,128)}, u32[]{:S(2)}, u32[]{:S(2)}) collective-permute-start(f32[3,40,4,128]{3,2,1,0:T(4,128)} %get-tuple-element.64), channel_id=1, source_target_pairs={{0,1},{1,0},{2,3},{3,2},{4,5},{5,4},{6,7},{7,6},{8,9},{9,8},{10,11... | collective-permute-start | bytes 737288 | tf_op jit(solution)/shard_map/ppermute | solution.py:21
  1161.3 28.2 %copy-start.4 = (f32[64,128,256]{2,1,0:T(8,128)}, f32[64,128,256]{2,1,0:T(8,128)S(1)}, u32[]{:S(2)}) copy-start(f32[64,128,256]{2,1,0:T(8,128)S(1)} %fusion.58) | copy-start | bytes 25165828
  1161.4 14.7 collective-permute-start.9
  1174.9 4.9 collective-permute-start.8
  1179.9 4.4 collective-permute-start.11
  1180.3 5.6 collective-permute-start.10
  1278.7 16.3 copy-start.28
  1378.9 37.7 %slice-start.5 = ((s8[6291456]{0:T(1024)(128)(4,1)}), s8[4194304]{0:T(1024)(128)(4,1)S(1)}, s32[]{:S(2)}) async-start(s8[6291456]{0:T(1024)(128)(4,1)} %bitcast.192), calls=%async_computation.9 | async-start | bytes 8388608
  1378.9 37.7 %slice-start.6 = ((s8[6291456]{0:T(1024)(128)(4,1)}), s8[2097152]{0:T(1024)(128)(4,1)S(1)}, s32[]{:S(2)}) async-start(s8[6291456]{0:T(1024)(128)(4,1)} %bitcast.192), calls=%async_computation.10 | async-start | bytes 4194304
  1402.8 18.0 copy-start.3
  1402.9 9.5 collective-permute-start.13
  1411.2 3.7 collective-permute-start.12
  1415.1 4.4 collective-permute-start.15
  1415.4 5.3 collective-permute-start.14
  1513.3 16.3 copy-start.26
  1611.8 33.2 %copy-start.30 = (s32[256]{0:T(256)S(1)}, s32[256]{0:T(256)}, u32[]{:S(2)}) copy-start(s32[256]{0:T(256)} %copy-done.29) | copy-start | bytes 3076
  1639.5 10.9 copy-start.20
  2046.3 27.5 %slice-start.1 = ((s8[6291456]{0:T(1024)(128)(4,1)}), s8[4194304]{0:T(1024)(128)(4,1)S(1)}, s32[]{:S(2)}) async-start(s8[6291456]{0:T(1024)(128)(4,1)} %bitcast.179), calls=%async_computation.5 | async-start | bytes 8388608
  2046.3 27.5 %slice-start.2 = ((s8[6291456]{0:T(1024)(128)(4,1)}), s8[2097152]{0:T(1024)(128)(4,1)S(1)}, s32[]{:S(2)}) async-start(s8[6291456]{0:T(1024)(128)(4,1)} %bitcast.179), calls=%async_computation.6 | async-start | bytes 4194304
  2103.1 28.2 %slice-start.3 = ((s8[6291456]{0:T(1024)(128)(4,1)}), s8[4194304]{0:T(1024)(128)(4,1)S(1)}, s32[]{:S(2)}) async-start(s8[6291456]{0:T(1024)(128)(4,1)} %bitcast.187), calls=%async_computation.7 | async-start | bytes 8388608
  2103.1 28.2 %slice-start.4 = ((s8[6291456]{0:T(1024)(128)(4,1)}), s8[2097152]{0:T(1024)(128)(4,1)S(1)}, s32[]{:S(2)}) async-start(s8[6291456]{0:T(1024)(128)(4,1)} %bitcast.187), calls=%async_computation.8 | async-start | bytes 4194304
  (28 other events, 188.5 us)
where the time goes:
time: 2170 us; the launch traced here: 2150 us
  other arithmetic  660 us (30%)
  local copies, waits for them, and re-layouts  577 us (27%)
  waiting for transfers between devices  377 us (17%)
  matrix products  232 us (11%)
  blocking collectives  223 us (10%)
  starting transfers between devices  78.7 us (4%)
    dot_general x22, matrix products, contract(): return jnp.einsum(form, left, right, precision=lax.Precision.HIGHEST)  232 us
    all_to_all x1, waiting for transfers between devices, across_px(): return lax.all_to_all(pieces, 'px', split_axis=2, concat_axis=1, tiled=True)  224 us
    sub x6, other arithmetic, divergence(): jnp.maximum(face, 0.0) * left + jnp.minimum(face, 0.0) * right  153 us
    all_to_all x1, blocking collectives, across_px(): return lax.all_to_all(pieces, 'px', split_axis=2, concat_axis=1, tiled=True)  150 us
    mul x9, other arithmetic, limited_slope(): 0.5 * (jnp.sign(first) + jnp.sign(second))  128 us
    ppermute x8, waiting for transfers between devices, padded(): lax.ppermute(lax.slice_in_dim(block, 0, width, axis=dim), axis, backward)  117 us
    slice x5, local copies, waits for them, and re-layouts, body(): ordered[1]  95.5 us
    sub x3, other arithmetic, spin_divergence(): jnp.maximum(face, 0.0) * left + jnp.minimum(face, 0.0) * right  82.7 us
  transfers between devices with their start and end apart: 18, of which 13 were waited for; matrix products, arithmetic and copies ran while one was open for 5% of the time, Pallas kernels for 0%

commit v1 on v0

--- a/solution.py
+++ b/solution.py
@@ -3,6 +3,8 @@
 import jax
 import jax.numpy as jnp
 from jax import lax
+from jax.experimental import pallas as pl
+from jax.experimental.pallas import tpu as pltpu
 from jax.sharding import PartitionSpec as P
 
 NSUB = 3
@@ -12,8 +14,8 @@
 DIFFUSION_RATIO = 1.0
 
 
-def padded(block, sides, width):
-    for axis, dim in sides:
+def padded(block, sides):
+    for axis, dim, width in sides:
         count = lax.axis_size(axis)
         forward = [(i, i + 1) for i in range(count - 1)]
         forward.append((count - 1, 0))
@@ -27,7 +29,7 @@
 
 
 def contract(form, left, right):
-    return jnp.einsum(form, left, right, precision=lax.Precision.HIGHEST)
+    return jnp.einsum(form, left, right, precision=lax.Precision.HIGH)
 
 
 def dft_table(length, sign):
@@ -78,58 +80,190 @@
     return lax.all_to_all(pieces, "py", split_axis=2, concat_axis=1, tiled=True)
 
 
-def slab(array, start, stop, axis):
-    return lax.slice_in_dim(array, start, stop, axis=axis)
-
-
-def refine(field, axis):
-    count = field.shape[axis]
-    points = slab(field, 2, count - 1, axis)
-    middles = (
-        9.0 * (slab(field, 1, count - 2, axis) + points)
-        - (slab(field, 0, count - 3, axis) + slab(field, 3, count, axis))
-    ) / 16.0
-    paired = jnp.concatenate([middles, points], axis=axis + 1)
-    shape = list(field.shape)
-    shape[axis] = 2 * (count - 3)
-    return paired.reshape(shape)
-
-
-def limited_slope(first, second):
-    return 0.5 * (jnp.sign(first) + jnp.sign(second)) * jnp.minimum(jnp.abs(first), jnp.abs(second))
-
-
-def spin_divergence(theta, speed, axis):
-    ahead = jnp.roll(theta, -1, axis)
-    jump = ahead - theta
-    slope = limited_slope(jnp.roll(jump, 1, axis), jump)
-    left = theta + 0.5 * slope
-    right = ahead - 0.5 * jnp.roll(slope, -1, axis)
-    face = 0.5 * (speed + jnp.roll(speed, -1, axis))
-    flux = jnp.maximum(face, 0.0) * left + jnp.minimum(face, 0.0) * right - DIFFUSION_RATIO * jump
-    return flux - jnp.roll(flux, 1, axis)
-
-
-def divergence(theta, speed, axis):
-    count = theta.shape[axis]
-    jump = slab(theta, 1, count, axis) - slab(theta, 0, count - 1, axis)
-    slope = limited_slope(slab(jump, 0, count - 2, axis), slab(jump, 1, count - 1, axis))
-    left = slab(theta, 1, count - 2, axis) + 0.5 * slab(slope, 0, count - 3, axis)
-    right = slab(theta, 2, count - 1, axis) - 0.5 * slab(slope, 1, count - 2, axis)
-    face = 0.5 * (slab(speed, 0, count - 3, axis) + slab(speed, 1, count - 2, axis))
-    flux = (
-        jnp.maximum(face, 0.0) * left
-        + jnp.minimum(face, 0.0) * right
-        - DIFFUSION_RATIO * slab(jump, 1, count - 2, axis)
-    )
-    return slab(flux, 1, count - 3, axis) - slab(flux, 0, count - 4, axis)
-
-
-def advance(theta, speed):
-    flow_first = divergence(theta[:, 1:-1], speed[0], 0)[:, 1:-1]
-    flow_second = divergence(theta[1:-1, :], speed[1], 1)[1:-1, :]
-    flow_third = spin_divergence(theta[1:-1, 1:-1], speed[2], 2)[1:-1, 1:-1]
-    return theta[2:-2, 2:-2] - STEP_RATIO * (flow_first + flow_second + flow_third)
+ROW_PAD = 8
+
+
+def refine_rows(points):
+    rows = jnp.arange(2 * points, dtype=jnp.int32)[:, None]
+    cols = jnp.arange(points, dtype=jnp.int32)[None, :]
+
+    def weights(row):
+        half = row // 2
+        gap = cols - half
+        near = jnp.logical_or(gap == 0, gap == 1)
+        distant = jnp.logical_or(gap == -1, gap == 2)
+        odd = jnp.where(near, 9.0 / 16.0, 0.0) - jnp.where(distant, 1.0 / 16.0, 0.0)
+        return jnp.where(row % 2 == 1, odd, jnp.where(gap == 0, 1.0, 0.0))
+
+    cell = weights(rows)
+    return cell, 0.5 * (cell + weights(rows + 1))
+
+
+def split(value):
+    high = value.astype(jnp.bfloat16)
+    return high, (value - high.astype(jnp.float32)).astype(jnp.bfloat16)
+
+
+def table_right(value, table):
+    high, low = split(value)
+    return jnp.dot(high, table, preferred_element_type=jnp.float32) + jnp.dot(
+        low, table, preferred_element_type=jnp.float32
+    )
+
+
+def table_left(table, value):
+    high, low = split(value)
+    return jnp.dot(table, high, preferred_element_type=jnp.float32) + jnp.dot(
+        table, low, preferred_element_type=jnp.float32
+    )
+
+
+def half_slope(first, second):
+    low = jnp.minimum(first, second)
+    high = jnp.maximum(first, second)
+    return 0.5 * (jnp.maximum(low, 0.0) + jnp.minimum(high, 0.0))
+
+
+def upwind(face, left, right, jump):
+    return face * jnp.where(face > 0.0, left, right) - DIFFUSION_RATIO * jump
+
+
+def line_div(theta, face, axis):
+    size = theta.shape[axis]
+    jump = pltpu.roll(theta, size - 1, axis) - theta
+    slope = half_slope(pltpu.roll(jump, 1, axis), jump)
+    right = pltpu.roll(theta - slope, size - 1, axis)
+    flux = upwind(face, theta + slope, right, jump)
+    return flux - pltpu.roll(flux, 1, axis)
+
+
+def substep(prev, new, slope_ref, flux_ref, fx, fy, fz, store, first, count, chunk):
+    def run(index, carry):
+        row = pl.multiple_of(first + index * chunk, 8)
+        here = pl.ds(row, chunk)
+        inner = pl.ds(pl.multiple_of(row + ROW_PAD, 8), chunk)
+        wide = pl.ds(row, chunk + 2 * ROW_PAD)
+        b0 = prev[0, inner]
+        b1 = prev[1, inner]
+        a0 = new[0, inner]
+        a1 = new[1, inner]
+        jump_b = b1 - b0
+        jump_m = a0 - b1
+        slope_b = half_slope(jump_b, jump_m)
+        slope_a = half_slope(jump_m, a1 - a0)
+        flux_0 = upwind(fx[0, here], b0 + slope_ref[here], b1 - slope_b, jump_b)
+        flux_1 = upwind(fx[1, here], b1 + slope_b, a0 - slope_a, jump_m)
+        div_0 = flux_0 - flux_ref[here]
+        div_1 = flux_1 - flux_0
+        slope_ref[here] = slope_a
+        flux_ref[here] = flux_1
+        for plane, (base, div) in enumerate(((b0, div_0), (b1, div_1))):
+            side = line_div(prev[plane, wide], fy[plane, wide], 0)
+            side = side[ROW_PAD : ROW_PAD + chunk]
+            total = div + side + line_div(base, fz[plane, here], 1)
+            store(plane, row, base - STEP_RATIO * total)
+        return carry
+
+    lax.fori_loop(0, count, run, 0)
+
+
+def march(
+    theta_ref, speed_ref, my_ref, myf_ref, mz_ref, mzf_ref, py_ref, pz_ref,
+    out_ref, pool_ref, t0, t1, t2, slopes, fluxes, fx, fy, fz,
+):
+    step = pl.program_id(0)
+    now = lax.rem(step, 2)
+    old = 1 - now
+    rows = theta_ref.shape[1]
+    inner = pl.ds(ROW_PAD, rows)
+    t0[now, 0, inner] = theta_ref[0]
+    t0[now, 1, inner] = theta_ref[1]
+    slot = lax.rem(step, 3)
+    before = lax.rem(step + 2, 3)
+    oldest = lax.rem(step + 1, 3)
+    for part in range(3):
+        q0 = speed_ref[part, step]
+        q1 = speed_ref[part, step + 1]
+        qm = speed_ref[part, jnp.maximum(step - 1, 0)]
+        q2 = speed_ref[part, step + 2]
+        odd = (9.0 * (q0 + q1) - (qm + q2)) * (1.0 / 16.0)
+        pair = (0.5 * (q0 + odd), 0.5 * (odd + q1)) if part == 0 else (q0, odd)
+        for plane in range(2):
+            line = table_right(pair[plane], (mzf_ref if part == 2 else mz_ref)[...])
+            full = table_left((myf_ref if part == 1 else my_ref)[...], line)
+            if part == 1:
+                fy[slot, plane, inner] = full
+            else:
+                (fx if part == 0 else fz)[slot, plane] = full
+    whole = rows // 24 if rows % 24 == 0 else rows // 8
+    chunk = rows // whole
+
+    def keep(target):
+        def store(plane, row, value):
+            target[now, plane, pl.ds(pl.multiple_of(row + ROW_PAD, 8), value.shape[0])] = value
+
+        return store
+
+    def emit(plane, row, value):
+        out_ref[plane, pl.ds(pl.multiple_of(row - ROW_PAD, 8), value.shape[0])] = value
+
+    substep(
+        t0.at[old], t0.at[now], slopes.at[0], fluxes.at[0],
+        fx.at[slot], fy.at[slot], fz.at[slot], keep(t1), 0, whole, chunk,
+    )
+    substep(
+        t1.at[old], t1.at[now], slopes.at[1], fluxes.at[1],
+        fx.at[before], fy.at[before], fz.at[before], keep(t2), 0, whole, chunk,
+    )
+    last = rows - 2 * ROW_PAD
+    last_chunk = 32 if last % 32 == 0 else 8
+    substep(
+        t2.at[old], t2.at[now], slopes.at[2], fluxes.at[2],
+        fx.at[oldest], fy.at[oldest], fz.at[oldest], emit, ROW_PAD, last // last_chunk, last_chunk,
+    )
+    both = out_ref[0] + out_ref[1]
+    pool_ref[0] = table_left(py_ref[...], table_right(both, pz_ref[...]))
+
+
+def scalar_steps(grown, widened):
+    planes, rows, cells = grown.shape
+    wide_first, wide_second, third = widened.shape[1:]
+    steps = planes // 2
+    first = planes - 12
+    inner = rows - 2 * ROW_PAD
+    cell, face = refine_rows(wide_second)
+    up = upsample_table(third)
+    up_face = 0.5 * (up + jnp.roll(up, -1, axis=1))
+    pool_rows = (8.0 * pair_table(inner // 2)).T
+    tables = [cell, face, up, up_face, pool_rows, pair_table(third)]
+    tables = [table.astype(jnp.bfloat16) for table in tables]
+    tall = rows + 2 * ROW_PAD
+    f32 = jnp.float32
+    return pl.pallas_call(
+        march,
+        grid=(steps,),
+        in_specs=[
+            pl.BlockSpec((2, rows, cells), lambda g: (g, 0, 0)),
+            pl.BlockSpec((3, wide_first, wide_second, third), lambda g: (0, 0, 0, 0)),
+        ]
+        + [pl.BlockSpec(table.shape, lambda g: (0, 0)) for table in tables],
+        out_specs=[
+            pl.BlockSpec((2, inner, cells), lambda g: (jnp.maximum(g - 6, 0), 0, 0)),
+            pl.BlockSpec((1, inner // 2, third), lambda g: (jnp.maximum(g - 6, 0), 0, 0)),
+        ],
+        out_shape=[
+            jax.ShapeDtypeStruct((first, inner, cells), f32),
+            jax.ShapeDtypeStruct((first // 2, inner // 2, third), f32),
+        ],
+        scratch_shapes=[pltpu.VMEM((2, 2, tall, cells), f32)] * 3
+        + [pltpu.VMEM((3, rows, cells), f32)] * 2
+        + [
+            pltpu.VMEM((3, 2, rows, cells), f32),
+            pltpu.VMEM((3, 2, tall, cells), f32),
+            pltpu.VMEM((3, 2, rows, cells), f32),
+        ],
+        compiler_params=pltpu.CompilerParams(dimension_semantics=("arbitrary",)),
+    )(grown, widened, *tables)
 
 
 def body(spectrum, scalar):
@@ -201,19 +335,9 @@
     ) * factor
     velocity = physical[:3]
     vorticity = physical[3:]
-    widened = padded(velocity, (("px", 1), ("py", 2)), 4)
-    speed = contract("cxyz,zw->cxyw", widened, upsample_table(length_third))
-    speed = refine(speed, 1)
-    speed = refine(speed, 2)
-    theta = scalar
-    inner_speed = speed[:, 4:-4, 4:-4]
-    for turn in range(NSUB):
-        grown = padded(theta, (("px", 0), ("py", 1)), 2)
-        theta = advance(grown, inner_speed)
-    pair_first = theta.reshape(cells_first, 2, 2 * cells_second, 2 * length_third).sum(axis=1)
-    pair_both = pair_first.reshape(cells_first, cells_second, 4 * length_third)
-    pair_both = pair_both[..., : 2 * length_third] + pair_both[..., 2 * length_third :]
-    buoyancy = contract("xyw,wz->xyz", pair_both, pair_table(length_third))
+    widened = padded(velocity, (("px", 1, 4), ("py", 2, 4)))
+    grown = padded(scalar, (("px", 0, 6), ("py", 1, ROW_PAD)))
+    theta, buoyancy = scalar_steps(grown, widened)
     forcing = jnp.stack(
         [
             velocity[1] * vorticity[2] - velocity[2] * vorticity[1],

time: 2170 us -> 1490 us (0.69)
  other arithmetic: 660 us -> 49.7 us
  Pallas kernels: 0 us -> 250 us
  local copies, waits for them, and re-layouts: 577 us -> 374 us
  matrix products: 232 us -> 149 us
  waiting for transfers between devices: 377 us -> 335 us
  blocking collectives: 223 us -> 260 us
  starting transfers between devices: 78.7 us -> 53 us
    sub x20 -> x0, other arithmetic: 374 us -> none  [the longest x6 153 us: divergence(): jnp.maximum(face, 0.0) * left + jnp.minimum(face, 0.0) * right]
    pallas_call x0 -> x1, Pallas kernels: none -> 250 us  [scalar_steps(): pl.pallas_call(march, grid=(steps,), in_specs=[pl.BlockSpec((2, rows, cel...]
    slice x27 -> x2, local copies, waits for them, and re-layouts: 146 us -> 0.09 us  [scalar_steps(): up_face = 0.5 * (up + jnp.roll(up, -1, axis=1))]
    mul x9 -> x0, other arithmetic: 128 us -> none  [limited_slope(): 0.5 * (jnp.sign(first) + jnp.sign(second))]
    ppermute x8 -> x4, waiting for transfers between devices: 117 us -> 2.64 us  [padded(): lax.ppermute(lax.slice_in_dim(block, 0, width, axis=dim), axis, backward)]
    dot_general x22 -> x20, matrix products: 232 us -> 149 us  [contract(): return jnp.einsum(form, left, right, precision=lax.Precision.HIGH)]
    all_to_all x1, waiting for transfers between devices: 0.01 us -> 72 us  [across_py(): return lax.all_to_all(pieces, 'py', split_axis=2, concat_axis=1, tiled=True)]
    all_to_all x1, blocking collectives: 150 us -> 214 us  [across_px(): return lax.all_to_all(pieces, 'px', split_axis=2, concat_axis=1, tiled=True)]
  transfers between devices with their start and end apart: 18 -> 10, of which waited for: 13 -> 5; matrix products, arithmetic and copies ran while one was open for 5% -> 11% of each run, Pallas kernels for 0% -> 0%
where the time goes in v1:
time: 1490 us; the launch traced here: 1470 us
  local copies, waits for them, and re-layouts  374 us (25%)
  waiting for transfers between devices  335 us (22%)
  blocking collectives  260 us (17%)
  Pallas kernels  250 us (17%)
  matrix products  149 us (10%)
  starting transfers between devices  53 us (4%)
  other arithmetic  49.7 us (3%)
    pallas_call x1, Pallas kernels, scalar_steps(): pl.pallas_call(march, grid=(steps,), in_specs=[pl.BlockSpec((2, rows, cel...  250 us
    all_to_all x1, waiting for transfers between devices, across_px(): return lax.all_to_all(pieces, 'px', split_axis=2, concat_axis=1, tiled=True)  224 us
    all_to_all x1, blocking collectives, across_px(): return lax.all_to_all(pieces, 'px', split_axis=2, concat_axis=1, tiled=True)  214 us
    dot_general x20, matrix products, contract(): return jnp.einsum(form, left, right, precision=lax.Precision.HIGH)  149 us
    slice x5, local copies, waits for them, and re-layouts, body(): ordered[1]  95.5 us
    all_to_all x1, waiting for transfers between devices, across_py(): return lax.all_to_all(pieces, 'py', split_axis=2, concat_axis=1, tiled=True)  72 us
    all_to_all x1, blocking collectives, across_py(): return lax.all_to_all(pieces, 'py', split_axis=2, concat_axis=1, tiled=True)  45.8 us
    slice x2, local copies, waits for them, and re-layouts, body(): ordered[0]  37.9 us
  transfers between devices with their start and end apart: 10, of which 5 were waited for; matrix products, arithmetic and copies ran while one was open for 11% of the time, Pallas kernels for 0%

profile of v1, /device:TPU:1, one launch (start us, length us, event | category | flops | bytes accessed | tf_op | source)
XLA Modules:
  0.0 1472.9 jit_solution(9441129685779856860)
XLA Ops:
  8.4 10.1 fusion.17
  18.5 10.2 fusion.21
  29.3 10.7 add_bitcast_fusion.1
  39.9 10.5 subtract_bitcast_fusion.1
  56.5 12.2 copy.37
  76.1 224.1 %all-to-all-done = f32[2,8,512,320]{3,1,0,2:T(8,128)} async-done(((f32[2,8,512,320]{3,1,0,2:T(8,128)}), f32[2,8,512,320]{3,1,0,2:T(8,128)}, u32[]{:S(2)}, u32[]{:S(2)}) %all-to-all-start) | async-done | bytes 10485792 | tf_op jit(solution)/shard_map/all_to_all | solution.py:76
  300.3 13.2 copy.38
  366.8 10.7 maximum_bitcast_fusion
  377.4 16.4 %copy.45 = f32[2,1,128,32,384]{4,3,0,1,2:T(8,128)} copy(f32[2,1,128,32,384]{4,2,3,0,1:T(8,128)} %maximum_bitcast_fusion) | data formatting | bytes 25165824 | tf_op jit(solution)/shard_map/broadcast_in_dim | solution.py:326
  403.8 16.6 %collective-permute-start = (f32[6,128,256]{2,1,0:T(8,128)S(1)}, f32[6,128,256]{2,1,0:T(8,128)S(1)}, u32[]{:S(2)}, u32[]{:S(2)}) collective-permute-start(f32[6,128,256]{2,1,0:T(8,128)S(1)} %get-tuple-element.25), channel_id=1, source_target_pairs={{0,2},{2,4},{4,6},{6,8},{8,10},{10,12},{12,14},{14,16},{16,18},{18... | collective-permute-start | bytes 2359304 | tf_op jit(solution)/shard_map/ppermute | solution.py:23
  423.5 33.6 %collective-permute-done = f32[6,128,256]{2,1,0:T(8,128)S(1)} collective-permute-done((f32[6,128,256]{2,1,0:T(8,128)S(1)}, f32[6,128,256]{2,1,0:T(8,128)S(1)}, u32[]{:S(2)}, u32[]{:S(2)}) %collective-permute-start) | collective-permute-done | bytes 786464 | tf_op jit(solution)/shard_map/ppermute | solution.py:23
  468.1 72.0 %all-to-all-done.1 = f32[2,1,128,32,384]{4,3,0,1,2:T(8,128)} async-done(((f32[2,1,128,32,384]{4,3,0,1,2:T(8,128)}), f32[2,1,128,32,384]{4,3,0,1,2:T(8,128)}, u32[]{:S(2)}, u32[]{:S(2)}) %all-to-all-start.1) | async-done | bytes 12582944 | tf_op jit(solution)/shard_map/all_to_all | solution.py:80
  540.1 12.7 copy.46
  552.7 24.7 %reshape.390 = f32[2,2,64,32,6,64]{2,1,5,4,3,0:T(2,128)} reshape(f32[2,1,128,32,384]{2,4,3,0,1:T(8,128)} %copy.46) | data formatting | bytes 25165824 | tf_op jit(solution)/shard_map/reshape | solution.py:327
  577.4 25.1 %fusion.200 = (f32[1,6,32,64,2,64]{3,4,5,1,2,0:T(2,128)}, f32[1,6,32,64,2,64]{3,4,5,1,2,0:T(2,128)}) fusion(f32[2,6,32,64,2,64]{3,4,5,1,2,0:T(2,128)} %bitcast.140), kind=kLoop, calls=%fused_computation.279 | loop fusion | bytes 25165824 | tf_op jit(solution)/shard_map/slice | solution.py:334
  602.5 22.8 %copy.48 = f32[1,6,32,64,2,64]{5,4,3,2,1,0:T(2,128)} copy(f32[1,6,32,64,2,64]{3,4,5,1,2,0:T(2,128)} %get-tuple-element.10) | data formatting | bytes 12582912 | tf_op jit(solution)/shard_map/slice | solution.py:334
  625.4 12.7 squeeze.47
  638.1 22.8 %copy.47 = f32[1,6,32,64,2,64]{5,4,3,2,1,0:T(2,128)} copy(f32[1,6,32,64,2,64]{3,4,5,1,2,0:T(2,128)} %get-tuple-element.11) | data formatting | bytes 12582912 | tf_op jit(solution)/shard_map/slice | solution.py:333
  660.9 12.7 squeeze.46
  684.1 17.4 %collective-permute-start.4 = (f32[3,4,64,128]{3,2,1,0:T(8,128)}, f32[3,4,64,128]{3,2,1,0:T(8,128)S(1)}, u32[]{:S(2)}, u32[]{:S(2)}) collective-permute-start(f32[3,4,64,128]{3,2,1,0:T(8,128)} %get-tuple-element.30), channel_id=1, source_target_pairs={{0,2},{2,4},{4,6},{6,8},{8,10},{10,12},{12,14},{14,16},{16,18},{18... | collective-permute-start | bytes 1179656 | tf_op jit(solution)/shard_map/ppermute | solution.py:23
  722.0 250.3 %shard_map.41 = (f32[64,128,256]{2,1,0:T(8,128)}, f32[32,64,128]{2,1,0:T(8,128)}) custom-call(f32[76,144,256]{2,1,0:T(8,128)} %pad_maximum_fusion.theta_ref, f32[3,40,72,128]{3,2,1,0:T(8,128)} %pad_maximum_fusion.4.speed_ref, bf16[144,72]{1,0:T(8,128)(2,1)} %get-tuple-element.41.my_ref, bf16[144,72]{1,0:T(8,128)(2,1)} %get-tuple-element.40.myf_ref, ...), custom_call_target="tpu_custom_call" | custom-call | tf_op jit(solution)/shard_map/pallas_call | solution.py:242
  987.6 45.8 %all_to_all.42 = f32[2,1,128,6144]{3,0,1,2:T(2,128)} all-to-all(f32[2,1,128,6144]{3,0,1,2:T(2,128)} %copy.49), channel_id=1, replica_groups=mesh['px'=16,'py'=2] {'py'}, dimensions={2} | all-to-all | bytes 12582912 | tf_op jit(solution)/shard_map/all_to_all | solution.py:80
  1033.4 12.7 reshape.392
  1046.2 21.1 %copy.78 = f32[2,2,64,3,32,64]{5,1,4,3,2,0:T(2,128)S(1)} copy(f32[2,2,64,3,32,64]{5,4,3,0,2,1:T(8,128)} %reshape.392) | data formatting | bytes 12582912 | tf_op jit(solution)/shard_map/reshape | solution.py:354
  1106.9 214.3 %all_to_all.43 = f32[2,1,128,6144]{3,0,1,2:T(2,128)S(1)} all-to-all(f32[2,1,128,6144]{3,0,1,2:T(2,128)} %copy.51), channel_id=1, replica_groups=mesh['px'=16,'py'=2] {'px'}, dimensions={2} | all-to-all | bytes 12582912 | tf_op jit(solution)/shard_map/all_to_all | solution.py:76
  1327.5 31.2 %reshape.393 = f32[2,16,8,64,3,32]{5,4,3,2,1,0:T(4,128)} reshape(f32[2,1,128,6144]{3,2,0,1:T(8,128)} %copy.52) | data formatting | bytes 12582912 | tf_op jit(solution)/shard_map/reshape | solution.py:361
  1358.7 25.7 %fusion.199 = (f32[1,3,8,64,16,32]{5,1,3,2,4,0:T(4,128)}, f32[1,3,8,64,16,32]{5,1,3,2,4,0:T(4,128)}) fusion(f32[2,3,8,64,16,32]{5,1,3,2,4,0:T(4,128)} %bitcast.139), kind=kLoop, calls=%fused_computation.278 | loop fusion | bytes 12582912 | tf_op jit(solution)/shard_map/slice | solution.py:366
  1384.4 15.1 %copy.53 = f32[1,3,8,64,16,32]{3,5,4,2,1,0:T(8,128)} copy(f32[1,3,8,64,16,32]{5,1,3,2,4,0:T(4,128)} %get-tuple-element.9) | data formatting | bytes 6291456 | tf_op jit(solution)/shard_map/slice | solution.py:366
  1399.5 11.8 fusion.13
  1411.4 14.9 %fusion.11 = f32[3,8,64,512]{3,2,1,0:T(8,128)} fusion(f32[3,8,64,512]{2,3,1,0:T(8,128)S(1)} %bitcast.144), kind=kOutput, calls=%fused_computation.52 | convolution fusion | flops 2419589120 | bytes 6291456 | tf_op jit(solution)/shard_map/cqsx,xk->cqsk/dot_general | solution.py:32
  1426.2 14.9 %copy.55 = f32[1,3,8,64,16,32]{3,5,4,2,1,0:T(8,128)} copy(f32[1,3,8,64,16,32]{5,1,3,2,4,0:T(4,128)} %get-tuple-element.8) | data formatting | bytes 6291456 | tf_op jit(solution)/shard_map/slice | solution.py:366
  1441.2 18.7 %subtract_bitcast_fusion.2 = f32[1,3,8,64,512]{4,3,2,1,0:T(8,128)S(1)} fusion(f32[3,8,64,512]{3,2,1,0:T(8,128)} %fusion.11, f32[3,8,64,512]{2,3,1,0:T(8,128)} %bitcast.149), kind=kOutput, calls=%fused_computation.27 | convolution fusion | flops 2420637696 | bytes 9437184 | tf_op jit(solution)/shard_map/cqsx,xk->cqsk/dot_general | solution.py:32
  (111 shorter events, 203.6 us)
Async XLA Ops:
  0.7 4.6 copy-start.10
  68.7 231.6 %all-to-all-start = ((f32[2,8,512,320]{3,1,0,2:T(8,128)}), f32[2,8,512,320]{3,1,0,2:T(8,128)}, u32[]{:S(2)}, u32[]{:S(2)}) async-start(f32[2,8,512,320]{3,1,0,2:T(8,128)} %copy.37), calls=%async_computation | async-start | bytes 25165824 | tf_op jit(solution)/shard_map/all_to_all | solution.py:76
  325.7 2.8 copy-start.2
  339.0 7.5 copy-start.7
  339.0 7.5 copy-start.8
  339.0 7.5 copy-start.9
  346.5 4.3 copy-start.4
  346.5 4.3 copy-start.5
  350.9 8.7 copy-start.6
  393.8 146.2 %all-to-all-start.1 = ((f32[2,1,128,32,384]{4,3,0,1,2:T(8,128)}), f32[2,1,128,32,384]{4,3,0,1,2:T(8,128)}, u32[]{:S(2)}, u32[]{:S(2)}) async-start(f32[2,1,128,32,384]{4,3,0,1,2:T(8,128)} %copy.45), calls=%async_computation.1 | async-start | bytes 25165824 | tf_op jit(solution)/shard_map/all_to_all | solution.py:80
  403.7 58.8 %collective-permute-start.1 = (f32[6,128,256]{2,1,0:T(8,128)S(1)}, f32[6,128,256]{2,1,0:T(8,128)S(1)}, u32[]{:S(2)}, u32[]{:S(2)}) collective-permute-start(f32[6,128,256]{2,1,0:T(8,128)S(1)} %get-tuple-element.24), channel_id=1, source_target_pairs={{2,0},{4,2},{6,4},{8,6},{10,8},{12,10},{14,12},{16,14},{18,16},{20... | collective-permute-start | bytes 2359304 | tf_op jit(solution)/shard_map/ppermute | solution.py:26
  403.8 53.3 %collective-permute-start = (f32[6,128,256]{2,1,0:T(8,128)S(1)}, f32[6,128,256]{2,1,0:T(8,128)S(1)}, u32[]{:S(2)}, u32[]{:S(2)}) collective-permute-start(f32[6,128,256]{2,1,0:T(8,128)S(1)} %get-tuple-element.25), channel_id=1, source_target_pairs={{0,2},{2,4},{4,6},{6,8},{8,10},{10,12},{12,14},{14,16},{16,18},{18... | collective-permute-start | bytes 2359304 | tf_op jit(solution)/shard_map/ppermute | solution.py:23
  462.6 3.8 copy-start.11
  466.5 235.0 %collective-permute-start.2 = (f32[76,8,256]{2,1,0:T(8,128)S(1)}, f32[76,8,256]{2,1,0:T(8,128)S(1)}, u32[]{:S(2)}, u32[]{:S(2)}) collective-permute-start(f32[76,8,256]{2,1,0:T(8,128)S(1)} %get-tuple-element.22), channel_id=1, source_target_pairs={{0,1},{1,0},{2,3},{3,2},{4,5},{5,4},{6,7},{7,6},{8,9},{9,8},{10,11... | collective-permute-start | bytes 1867784 | tf_op jit(solution)/shard_map/ppermute | solution.py:23
  468.0 233.5 %collective-permute-start.3 = (f32[76,8,256]{2,1,0:T(8,128)S(1)}, f32[76,8,256]{2,1,0:T(8,128)S(1)}, u32[]{:S(2)}, u32[]{:S(2)}) collective-permute-start(f32[76,8,256]{2,1,0:T(8,128)S(1)} %get-tuple-element.23), channel_id=1, source_target_pairs={{1,0},{0,1},{3,2},{2,3},{5,4},{4,5},{7,6},{6,7},{9,8},{8,9},{11,10... | collective-permute-start | bytes 1867784 | tf_op jit(solution)/shard_map/ppermute | solution.py:26
  673.7 6.3 copy-start.3
  683.0 30.0 %copy-start = (f32[6,32,64,128]{3,2,1,0:T(8,128)}, f32[6,32,64,128]{3,2,1,0:T(8,128)S(1)}, u32[]{:S(2)}) copy-start(f32[6,32,64,128]{3,2,1,0:T(8,128)S(1)} %subtract_multiply_fusion) | copy-start | bytes 18874372
  684.1 27.3 %collective-permute-start.4 = (f32[3,4,64,128]{3,2,1,0:T(8,128)}, f32[3,4,64,128]{3,2,1,0:T(8,128)S(1)}, u32[]{:S(2)}, u32[]{:S(2)}) collective-permute-start(f32[3,4,64,128]{3,2,1,0:T(8,128)} %get-tuple-element.30), channel_id=1, source_target_pairs={{0,2},{2,4},{4,6},{6,8},{8,10},{10,12},{12,14},{14,16},{16,18},{18... | collective-permute-start | bytes 1179656 | tf_op jit(solution)/shard_map/ppermute | solution.py:23
  701.5 9.9 collective-permute-start.5
  711.5 5.1 collective-permute-start.6
  711.6 7.7 collective-permute-start.7
  1092.8 4.0 copy-start.12
  1399.5 11.8 slice-start
  1399.5 11.8 slice-start.1
  1441.1 18.7 %copy-start.1 = (f32[1,3,8,64,16,32]{3,5,4,2,1,0:T(8,128)S(1)}, f32[1,3,8,64,16,32]{3,5,4,2,1,0:T(8,128)}, u32[]{:S(2)}) copy-start(f32[1,3,8,64,16,32]{3,5,4,2,1,0:T(8,128)} %copy.55) | copy-start | bytes 9437188

commit v2 on v1

--- a/solution.py
+++ b/solution.py
@@ -73,11 +73,7 @@
 
 
 def across_px(pieces):
-    return lax.all_to_all(pieces, "px", split_axis=2, concat_axis=1, tiled=True)
-
-
-def across_py(pieces):
-    return lax.all_to_all(pieces, "py", split_axis=2, concat_axis=1, tiled=True)
+    return lax.all_to_all(pieces, "px", split_axis=0, concat_axis=0, tiled=True)
 
 
 ROW_PAD = 8
@@ -263,7 +259,187 @@
             pltpu.VMEM((3, 2, rows, cells), f32),
         ],
         compiler_params=pltpu.CompilerParams(dimension_semantics=("arbitrary",)),
+        cost_estimate=pl.CostEstimate(
+            flops=400 * NSUB * grown.size, bytes_accessed=400 * grown.size, transcendentals=0
+        ),
     )(grown, widened, *tables)
+
+
+def split_table(table):
+    high = lax.reduce_precision(table, exponent_bits=8, mantissa_bits=7)
+    return jnp.stack([high, table - high]).astype(jnp.bfloat16)
+
+
+def product(left, right):
+    total = jnp.dot(left[0], right[1], preferred_element_type=jnp.float32)
+    total += jnp.dot(left[1], right[0], preferred_element_type=jnp.float32)
+    return total + jnp.dot(left[0], right[0], preferred_element_type=jnp.float32)
+
+
+def to_physical(lines_ref, second_ref, third_ref, left_ref, right_ref, out_ref):
+    span = third_ref.shape[1]
+    k2 = second_ref[...]
+    k3 = third_ref[...]
+    groups, _, lines, part, _ = out_ref.shape
+    left = (left_ref[0], left_ref[1])
+    right = (right_ref[0], right_ref[1])
+    length = left_ref.shape[1] // 2
+    for x in range(lines):
+        real = lines_ref[0, :, x, :]
+        imag = lines_ref[1, :, x, :]
+        re = [real[:, i * span : (i + 1) * span] for i in range(5)]
+        im = [imag[:, i * span : (i + 1) * span] for i in range(5)]
+        omega_re = [
+            -(k2 * im[2] - k3 * im[1]),
+            -k3 * im[0] - re[4],
+            re[3] + k2 * im[0],
+        ]
+        omega_im = [
+            k2 * re[2] - k3 * re[1],
+            k3 * re[0] - im[4],
+            im[3] - k2 * re[0],
+        ]
+        whole = jnp.concatenate(
+            [
+                jnp.concatenate(re[:3] + omega_re, axis=1),
+                jnp.concatenate(im[:3] + omega_im, axis=1),
+            ],
+            axis=0,
+        )
+        turned = product(left, split(whole))
+        for field in range(6):
+            cut = slice(field * span, (field + 1) * span)
+            line = jnp.concatenate([turned[:length, cut], turned[length:, cut]], axis=1)
+            value = product(split(line), right)
+            for group in range(groups):
+                out_ref[group, field, x] = value[group * part : (group + 1) * part]
+
+
+def physical_parts(landed, wave_second, wave_third, groups, length_third, factor):
+    _, length_second, lines, wide = landed.shape
+    span = wave_third.shape[0]
+    block = 8
+    cos2, sin2 = dft_table(length_second, 1.0)
+    left = jnp.concatenate(
+        [jnp.concatenate([cos2, -sin2], axis=1), jnp.concatenate([sin2, cos2], axis=1)]
+    )
+    start = lax.axis_index("py") * span
+    cos3, sin3 = dft_table(length_third, 1.0)
+    right = factor * jnp.concatenate(
+        [
+            lax.dynamic_slice_in_dim(cos3, start, span),
+            -lax.dynamic_slice_in_dim(sin3, start, span),
+        ]
+    )
+    part = length_second // groups
+    return pl.pallas_call(
+        to_physical,
+        grid=(lines // block,),
+        in_specs=[
+            pl.BlockSpec((2, length_second, block, wide), lambda g: (0, 0, g, 0)),
+            pl.BlockSpec((length_second, 1), lambda g: (0, 0)),
+            pl.BlockSpec((1, span), lambda g: (0, 0)),
+            pl.BlockSpec((2,) + left.shape, lambda g: (0, 0, 0)),
+            pl.BlockSpec((2,) + right.shape, lambda g: (0, 0, 0)),
+        ],
+        out_specs=pl.BlockSpec(
+            (groups, 6, block, part, length_third), lambda g: (0, 0, g, 0, 0)
+        ),
+        out_shape=jax.ShapeDtypeStruct((groups, 6, lines, part, length_third), jnp.float32),
+        compiler_params=pltpu.CompilerParams(dimension_semantics=("arbitrary",)),
+    )(landed, wave_second[:, None], wave_third[None, :], split_table(left), split_table(right))
+
+
+def back_second(force_ref, table_ref, out_ref):
+    groups, fields, lines, _, both = force_ref.shape
+    span = both // 2
+    owners, _, _, rows, _ = out_ref.shape
+    table = (table_ref[0], table_ref[1])
+    length = table_ref.shape[1] // 2
+
+    def run(x, carry):
+        data = jnp.concatenate(
+            [
+                jnp.concatenate([force_ref[g, f, x] for g in range(groups)], axis=0)
+                for f in range(fields)
+            ],
+            axis=1,
+        )
+        turned = product(table, split(data))
+        for f in range(fields):
+            top = turned[:length, f * both : (f + 1) * both]
+            low = turned[length:, f * both : (f + 1) * both]
+            value = jnp.concatenate(
+                [top[:, :span] - low[:, span:], low[:, :span] + top[:, span:]], axis=1
+            )
+            for owner in range(owners):
+                out_ref[owner, x, f] = value[owner * rows : (owner + 1) * rows]
+        return carry
+
+    lax.fori_loop(0, lines, run, 0)
+
+
+def second_lines(arrived, owners):
+    groups, fields, lines, part, both = arrived.shape
+    length = groups * part
+    rows = length // owners
+    block = 8
+    cosine, sine = dft_table(length, -1.0)
+    table = split_table(jnp.concatenate([cosine, sine]))
+    return pl.pallas_call(
+        back_second,
+        grid=(lines // block,),
+        in_specs=[
+            pl.BlockSpec((groups, fields, block, part, both), lambda g: (0, 0, g, 0, 0)),
+            pl.BlockSpec(table.shape, lambda g: (0, 0, 0)),
+        ],
+        out_specs=pl.BlockSpec((owners, block, fields, rows, both), lambda g: (0, g, 0, 0, 0)),
+        out_shape=jax.ShapeDtypeStruct((owners, lines, fields, rows, both), jnp.float32),
+        compiler_params=pltpu.CompilerParams(dimension_semantics=("arbitrary",)),
+    )(arrived, table)
+
+
+def back_first(early_ref, late_ref, table_ref, out_ref):
+    owners, lines, _, rows, both = early_ref.shape
+    span = both // 2
+    length = owners * lines
+    early = pl.num_programs(0) - 1
+
+    def run(data_ref):
+        table = (table_ref[0], table_ref[1])
+        for q in range(rows):
+            data = data_ref[:, :, 0, q, :].reshape(length, both)
+            turned = product(split(data.T), table)
+            out_ref[0, 0, q] = turned[:span, :length] - turned[span:, length:]
+            out_ref[1, 0, q] = turned[:span, length:] + turned[span:, :length]
+
+    @pl.when(pl.program_id(0) < early)
+    def _():
+        run(early_ref)
+
+    @pl.when(pl.program_id(0) == early)
+    def _():
+        run(late_ref)
+
+
+def first_lines(early, late, factor):
+    owners, lines, fields, rows, both = early.shape
+    length = owners * lines
+    cosine, sine = dft_table(length, -1.0)
+    table = split_table(factor * jnp.concatenate([cosine, sine], axis=1))
+    block = (owners, lines, 1, rows, both)
+    return pl.pallas_call(
+        back_first,
+        grid=(fields + 1,),
+        in_specs=[
+            pl.BlockSpec(block, lambda f: (0, 0, jnp.minimum(f, fields - 1), 0, 0)),
+            pl.BlockSpec(block, lambda f: (0, 0, 0, 0, 0)),
+            pl.BlockSpec(table.shape, lambda f: (0, 0, 0)),
+        ],
+        out_specs=pl.BlockSpec((2, 1, rows, both // 2, length), lambda f: (0, f, 0, 0, 0)),
+        out_shape=jax.ShapeDtypeStruct((2, fields + 1, rows, both // 2, length), jnp.float32),
+        compiler_params=pltpu.CompilerParams(dimension_semantics=("arbitrary",)),
+    )(early, late, table)
 
 
 def body(spectrum, scalar):
@@ -274,8 +450,6 @@
     length_first = spectrum.shape[4]
     length_second = spec_second * groups_x
     length_third = spec_third * groups_y
-    cells_first = length_first // groups_x
-    cells_second = length_second // groups_y
     factor = 1.0 / math.sqrt(length_first * length_second * length_third)
     wave_first = wavenumbers(length_first)
     third_local = lax.dynamic_slice_in_dim(
@@ -294,81 +468,51 @@
         spec_second, 5 * spec_third, length_first
     )
     out_real, out_imag = complex_apply(real_lines, imag_lines, first_cos, first_sin, "qlk,kx->qxl")
-    landed = across_px(jnp.stack([out_real, out_imag]))
-    wave_second = wavenumbers(length_second)[:, None, None]
-    wave_third = third_local[None, None, :]
-    real_in = landed[0]
-    imag_in = landed[1]
-
-    def member(array, index):
-        return array[..., index * spec_third : (index + 1) * spec_third]
-
-    omega_real = [
-        -(wave_second * member(imag_in, 2) - wave_third * member(imag_in, 1)),
-        -wave_third * member(imag_in, 0) - member(real_in, 4),
-        member(real_in, 3) + wave_second * member(imag_in, 0),
-    ]
-    omega_imag = [
-        wave_second * member(real_in, 2) - wave_third * member(real_in, 1),
-        wave_third * member(real_in, 0) - member(imag_in, 4),
-        member(imag_in, 3) - wave_second * member(real_in, 0),
-    ]
-    arrived = jnp.stack(
-        [
-            jnp.concatenate([real_in[..., : 3 * spec_third]] + omega_real, axis=-1),
-            jnp.concatenate([imag_in[..., : 3 * spec_third]] + omega_imag, axis=-1),
-        ]
-    )
-    second_cos, second_sin = dft_table(length_second, 1.0)
-    out_real, out_imag = complex_apply(
-        arrived[0], arrived[1], second_cos, second_sin, "pxl,py->yxl"
-    )
-    arrived = across_py(jnp.stack([out_real, out_imag])[:, None])
-    ordered = arrived.reshape(2, groups_y, cells_second, cells_first, 6, spec_third)
-    ordered = jnp.transpose(ordered, (0, 4, 3, 2, 1, 5)).reshape(
-        2, 6, cells_first, cells_second, length_third
-    )
-    third_cos, third_sin = dft_table(length_third, 1.0)
-    physical = (
-        contract("cxyn,nz->cxyz", ordered[0], third_cos)
-        - contract("cxyn,nz->cxyz", ordered[1], third_sin)
-    ) * factor
+    landed = lax.all_to_all(
+        jnp.stack([out_real, out_imag]), "px", split_axis=2, concat_axis=1, tiled=True
+    )
+    parts = physical_parts(
+        landed, wavenumbers(length_second), third_local, groups_y, length_third, factor
+    )
+    physical = lax.all_to_all(parts, "py", split_axis=0, concat_axis=0, tiled=True).sum(axis=0)
     velocity = physical[:3]
     vorticity = physical[3:]
+    back_cos, back_sin = dft_table(length_third, -1.0)
+
+    def send_back(force):
+        pieces = []
+        for group in range(groups_y):
+            cut = slice(group * spec_third, (group + 1) * spec_third)
+            table = jnp.concatenate([back_cos[:, cut], back_sin[:, cut]], axis=1)
+            pieces.append(contract("cxyz,zn->cxyn", force, table))
+        arrived = lax.all_to_all(jnp.stack(pieces), "py", split_axis=0, concat_axis=0, tiled=True)
+        return second_lines(arrived, groups_x)
+
+    early = send_back(
+        jnp.stack(
+            [
+                velocity[1] * vorticity[2] - velocity[2] * vorticity[1],
+                velocity[2] * vorticity[0] - velocity[0] * vorticity[2],
+            ]
+        )
+    )
     widened = padded(velocity, (("px", 1, 4), ("py", 2, 4)))
     grown = padded(scalar, (("px", 0, 6), ("py", 1, ROW_PAD)))
+    widened, early = lax.optimization_barrier((widened, early))
+    early = across_px(early)
     theta, buoyancy = scalar_steps(grown, widened)
-    forcing = jnp.stack(
-        [
-            velocity[1] * vorticity[2] - velocity[2] * vorticity[1],
-            velocity[2] * vorticity[0] - velocity[0] * vorticity[2],
-            velocity[0] * vorticity[1] - velocity[1] * vorticity[0] + buoyancy,
-        ]
-    )
-    back_cos, back_sin = dft_table(length_third, -1.0)
-    force_lines = forcing.reshape(3 * cells_first * cells_second, length_third)
-    sectioned = jnp.stack(
-        [contract("lz,zn->nl", force_lines, back_cos), contract("lz,zn->nl", force_lines, back_sin)]
-    )
-    arrived = across_py(sectioned[:, None])
-    ordered = arrived.reshape(2, groups_y, spec_third, 3, cells_first, cells_second)
-    ordered = jnp.transpose(ordered, (0, 2, 3, 4, 1, 5)).reshape(
-        2, spec_third * 3 * cells_first, length_second
-    )
-    back_cos, back_sin = dft_table(length_second, -1.0)
-    out_real, out_imag = complex_apply(ordered[0], ordered[1], back_cos, back_sin, "ly,yp->pl")
-    arrived = across_px(jnp.stack([out_real, out_imag])[:, None])
-    ordered = arrived.reshape(2, groups_x, spec_second, spec_third, 3, cells_first)
-    ordered = jnp.transpose(ordered, (0, 4, 2, 3, 1, 5)).reshape(
-        2, 3, spec_second, spec_third, length_first
-    )
-    back_cos, back_sin = dft_table(length_first, -1.0)
-    out_real, out_imag = complex_apply(ordered[0], ordered[1], back_cos, back_sin, "cqsx,xk->cqsk")
-    tendency = jnp.stack([out_real, out_imag]) * factor
+    early, buoyancy = lax.optimization_barrier((early, buoyancy))
+    late = send_back(
+        (velocity[0] * vorticity[1] - velocity[1] * vorticity[0] + buoyancy)[None]
+    )
+    late = across_px(late)
+    tendency = first_lines(early, late, factor)
     return (tendency, theta)
 
 
 def solution(mesh):
     in_specs = (P(None, None, "px", "py", None), P("px", "py", None))
     out_specs = (P(None, None, "px", "py", None), P("px", "py", None))
-    return jax.shard_map(body, mesh=mesh, in_specs=in_specs, out_specs=out_specs, check_vma=False)
+    return jax.shard_map(
+        body, mesh=mesh, in_specs=in_specs, out_specs=out_specs, check_vma=False
+    )

time: 1490 us -> 1140 us (0.77)
  local copies, waits for them, and re-layouts: 374 us -> 46.8 us
  blocking collectives: 260 us -> 17.3 us
  waiting for transfers between devices: 335 us -> 477 us
  starting transfers between devices: 53 us -> 164 us
  matrix products: 149 us -> 44.6 us
  Pallas kernels: 250 us -> 319 us
    all_to_all x2 -> x1, blocking collectives: 260 us -> 17.3 us  [send_back(): lax.all_to_all(jnp.stack(pieces), 'py', split_axis=0, concat_axis=0, tile...]
    slice x12 -> x1, local copies, waits for them, and re-layouts: 150 us -> 0.09 us  [send_back(): table = jnp.concatenate([back_cos[:, cut], back_sin[:, cut]], axis=1)]
    all_to_all x2 -> x5, starting transfers between devices: 15.8 us -> 141 us  [the longest x2 120 us: across_px(): return lax.all_to_all(pieces, 'px', split_axis=0, concat_axis=0, tiled=True)]
    dot_general x20 -> x8, matrix products: 149 us -> 44.6 us  [contract(): return jnp.einsum(form, left, right, precision=lax.Precision.HIGH)]
    all_to_all x2 -> x5, waiting for transfers between devices: 296 us -> 394 us  [the longest x1 221 us: body(): lax.all_to_all(jnp.stack([out_real, out_imag]), 'px', split_axis=2, conca...]
    reshape x4 -> x0, local copies, waits for them, and re-layouts: 89.7 us -> none  [the longest x2 33.8 us: body(): arrived.reshape(2, groups_y, spec_third, 3, cells_first, cells_second)]
    pallas_call x0 -> x4, Pallas kernels: none -> 68.9 us  [the longest x1 27.3 us: physical_parts(): pl.pallas_call(to_physical, grid=(lines // block,), in_specs=[pl.BlockSpe...]
    squeeze x4 -> x0, local copies, waits for them, and re-layouts: 37.4 us -> none  [the longest x2 18.8 us: body(): ordered[1]]
  transfers between devices with their start and end apart: 10 -> 13, of which waited for: 5 -> 10; matrix products, arithmetic and copies ran while one was open for 11% -> 3% of each run, Pallas kernels for 0% -> 22%
where the time goes in v2:
time: 1140 us; the launch traced here: 1120 us
  waiting for transfers between devices  477 us (42%)
  Pallas kernels  319 us (28%)
  starting transfers between devices  164 us (14%)
  other arithmetic  52.8 us (5%)
  local copies, waits for them, and re-layouts  46.8 us (4%)
  matrix products  44.6 us (4%)
  blocking collectives  17.3 us (2%)
    pallas_call x1, Pallas kernels, scalar_steps(): pl.pallas_call(march, grid=(steps,), in_specs=[pl.BlockSpec((2, rows, cel...  250 us
    all_to_all x1, waiting for transfers between devices, body(): lax.all_to_all(jnp.stack([out_real, out_imag]), 'px', split_axis=2, conca...  221 us
    all_to_all x1, waiting for transfers between devices, body(): lax.all_to_all(parts, 'py', split_axis=0, concat_axis=0, tiled=True)  137 us
    all_to_all x2, starting transfers between devices, across_px(): return lax.all_to_all(pieces, 'px', split_axis=0, concat_axis=0, tiled=True)  120 us
    ppermute x4, waiting for transfers between devices, padded(): lax.ppermute(lax.slice_in_dim(block, block.shape[dim] - width, None, axis...  71.2 us
    dot_general x8, matrix products, contract(): return jnp.einsum(form, left, right, precision=lax.Precision.HIGH)  44.6 us
    all_to_all x2, waiting for transfers between devices, across_px(): return lax.all_to_all(pieces, 'px', split_axis=0, concat_axis=0, tiled=True)  35.3 us
    pallas_call x1, Pallas kernels, physical_parts(): pl.pallas_call(to_physical, grid=(lines // block,), in_specs=[pl.BlockSpe...  27.3 us
  transfers between devices with their start and end apart: 13, of which 10 were waited for; matrix products, arithmetic and copies ran while one was open for 3% of the time, Pallas kernels for 22%

profile of v2, /device:TPU:1, one launch (start us, length us, event | category | flops | bytes accessed | tf_op | source)
XLA Modules:
  0.0 1122.4 jit_solution(10819827475264263903)
XLA Ops:
  0.7 3.8 slice_bitcast_fusion
  8.4 10.1 fusion.8
  18.5 10.2 fusion.12
  29.3 10.5 add_bitcast_fusion
  39.8 10.5 subtract_bitcast_fusion
  50.3 6.1 pad_maximum_fusion.1
  56.3 12.2 %copy.13 = f32[2,8,512,320]{3,1,0,2:T(8,128)} copy(f32[2,8,512,320]{2,3,1,0:T(8,128)} %pad_maximum_fusion.1) | data formatting | bytes 20971520 | tf_op jit(solution)/shard_map/stack | solution.py:472
  68.5 7.3 all-to-all-start
  79.3 220.7 %all-to-all-done = f32[2,8,512,320]{3,1,0,2:T(8,128)} async-done(((f32[2,8,512,320]{3,1,0,2:T(8,128)}), f32[2,8,512,320]{3,1,0,2:T(8,128)}, u32[]{:S(2)}, u32[]{:S(2)}) %all-to-all-start) | async-done | bytes 10485792 | tf_op jit(solution)/shard_map/all_to_all | solution.py:471
  300.0 13.2 %copy.15 = f32[2,16,8,32,320]{4,3,2,1,0:T(8,128)} copy(f32[2,16,8,32,320]{4,2,0,3,1:T(8,128)} %bitcast.16) | data formatting | bytes 20971520 | tf_op jit(solution)/shard_map/all_to_all | solution.py:471
  313.2 27.3 %shard_map.41 = f32[2,6,32,64,128]{4,3,2,1,0:T(8,128)} custom-call(f32[2,128,32,320]{3,2,1,0:T(8,128)} %bitcast.86, f32[128,1]{1,0:T(8,128)} %fusion.48.second_ref, f32[1,64]{1,0:T(1,128)} %dynamic-slice_bitcast_fusion.1.third_ref, bf16[2,256,256]{2,1,0:T(8,128)(2,1)} %pad_maximum_fusion.14.left_ref, bf16[2,128,128]{2,1,0:T(8,128)(2,1)} %pad_maximum_fusion.20.right_ref), custom_call_target="tpu_custom_call" | custom-call | tf_op jit(solution)/shard_map/pallas_call | solution.py:335
  340.5 8.5 all-to-all-start.1
  349.4 137.4 %all-to-all-done.1 = f32[2,6,32,64,128]{4,3,2,1,0:T(8,128)} async-done(((f32[2,6,32,64,128]{4,3,2,1,0:T(8,128)}), f32[2,6,32,64,128]{4,3,2,1,0:T(8,128)}, u32[]{:S(2)}, u32[]{:S(2)}) %all-to-all-start.1) | async-done | bytes 12582944 | tf_op jit(solution)/shard_map/all_to_all | solution.py:477
  486.8 9.4 reduce_sum.9
  504.2 5.6 all-to-all-start.2
  511.4 17.1 %collective-permute-start = (f32[3,4,64,128]{3,2,1,0:T(8,128)S(1)}, f32[3,4,64,128]{3,2,1,0:T(8,128)S(1)}, u32[]{:S(2)}, u32[]{:S(2)}) collective-permute-start(f32[3,4,64,128]{3,2,1,0:T(8,128)S(1)} %get-tuple-element.20), channel_id=1, source_target_pairs={{0,2},{2,4},{4,6},{6,8},{8,10},{10,12},{12,14},{14,16},{16,18},{18... | collective-permute-start | bytes 1179656 | tf_op jit(solution)/shard_map/ppermute | solution.py:23
  534.3 28.9 %collective-permute-done = f32[3,4,64,128]{3,2,1,0:T(8,128)S(1)} collective-permute-done((f32[3,4,64,128]{3,2,1,0:T(8,128)S(1)}, f32[3,4,64,128]{3,2,1,0:T(8,128)S(1)}, u32[]{:S(2)}, u32[]{:S(2)}) %collective-permute-start) | collective-permute-done | bytes 393248 | tf_op jit(solution)/shard_map/ppermute | solution.py:23
  574.1 13.9 %shard_map.42 = f32[16,32,2,8,128]{4,3,2,1,0:T(8,128)} custom-call(f32[2,2,32,64,128]{4,3,2,1,0:T(8,128)} %all-to-all-done.2.force_ref, bf16[2,256,128]{2,1,0:T(8,128)(2,1)} %pad_maximum_fusion.19.table_ref), custom_call_target="tpu_custom_call" | custom-call | tf_op jit(solution)/shard_map/pallas_call | solution.py:389
  588.0 49.4 %all-to-all-start.3 = ((f32[16,32,2,8,128]{4,3,2,1,0:T(8,128)}), f32[16,32,2,8,128]{4,3,2,1,0:T(8,128)}, u32[]{:S(2)}, u32[]{:S(2)}) async-start(f32[16,32,2,8,128]{4,3,2,1,0:T(8,128)} %shard_map.42), calls=%async_computation.3 | async-start | bytes 8388608 | tf_op jit(solution)/shard_map/all_to_all | solution.py:76
  641.5 33.0 %collective-permute-done.4 = f32[6,128,256]{2,1,0:T(8,128)S(1)} collective-permute-done((f32[6,128,256]{2,1,0:T(8,128)S(1)}, f32[6,128,256]{2,1,0:T(8,128)S(1)}, u32[]{:S(2)}, u32[]{:S(2)}) %collective-permute-start.4) | collective-permute-done | bytes 786464 | tf_op jit(solution)/shard_map/ppermute | solution.py:23
  674.6 4.9 constant_dynamic-update-slice_fusion.1
  679.6 3.7 copy-done.1
  687.1 5.5 collective-permute-done.7
  692.6 6.7 collective-permute-done.6
  699.2 9.6 pad_maximum_fusion.theta_ref
  708.8 250.2 %shard_map.43 = (f32[64,128,256]{2,1,0:T(8,128)}, f32[32,64,128]{2,1,0:T(8,128)}) custom-call(f32[76,144,256]{2,1,0:T(8,128)} %pad_maximum_fusion.theta_ref, f32[3,40,72,128]{3,2,1,0:T(8,128)} %pad_maximum_fusion.2.speed_ref, bf16[144,72]{1,0:T(8,128)(2,1)} %get-tuple-element.45.my_ref, bf16[144,72]{1,0:T(8,128)(2,1)} %get-tuple-element.44.myf_ref, ...), custom_call_target="tpu_custom_call" | custom-call | flops 3361996800 | bytes 1120665600 | tf_op jit(solution)/shard_map/pallas_call | solution.py:238
  963.6 17.3 %all_to_all.43.force_ref = f32[2,1,32,64,128]{4,3,2,1,0:T(8,128)} all-to-all(f32[2,1,32,64,128]{4,3,2,1,0:T(8,128)S(1)} %pad_maximum_fusion.5), channel_id=1, replica_groups=mesh['px'=16,'py'=2] {'py'}, dimensions={0} | all-to-all | bytes 4194304 | tf_op jit(solution)/shard_map/all_to_all | solution.py:488
  980.9 12.4 %shard_map.44 = f32[16,32,1,8,128]{4,3,2,1,0:T(8,128)} custom-call(f32[2,1,32,64,128]{4,3,2,1,0:T(8,128)} %all_to_all.43.force_ref, bf16[2,256,128]{2,1,0:T(8,128)(2,1)} %pad_maximum_fusion.19.table_ref), custom_call_target="tpu_custom_call" | custom-call | tf_op jit(solution)/shard_map/pallas_call | solution.py:389
  993.3 70.6 %all-to-all-start.5 = ((f32[16,32,1,8,128]{4,3,2,1,0:T(8,128)}), f32[16,32,1,8,128]{4,3,2,1,0:T(8,128)S(1)}, u32[]{:S(2)}, u32[]{:S(2)}) async-start(f32[16,32,1,8,128]{4,3,2,1,0:T(8,128)} %shard_map.44), calls=%async_computation.5 | async-start | bytes 4194304 | tf_op jit(solution)/shard_map/all_to_all | solution.py:76
  1063.9 4.1 multiply_bitcast_fusion
  1070.0 35.3 %all-to-all-done.5.late_ref = f32[16,32,1,8,128]{4,3,2,1,0:T(8,128)S(1)} async-done(((f32[16,32,1,8,128]{4,3,2,1,0:T(8,128)}), f32[16,32,1,8,128]{4,3,2,1,0:T(8,128)S(1)}, u32[]{:S(2)}, u32[]{:S(2)}) %all-to-all-start.5) | async-done | bytes 2097184 | tf_op jit(solution)/shard_map/all_to_all | solution.py:76
  1106.7 15.3 %shard_map.45 = f32[2,3,8,64,512]{4,3,2,1,0:T(8,128)} custom-call(f32[16,32,2,8,128]{4,3,2,1,0:T(8,128)} %all-to-all-done.3.early_ref, f32[16,32,1,8,128]{4,3,2,1,0:T(8,128)} %copy-done.2, bf16[2,512,1024]{2,1,0:T(8,128)(2,1)} %pad_maximum_fusion.6.table_ref), custom_call_target="tpu_custom_call" | custom-call | tf_op jit(solution)/shard_map/pallas_call | solution.py:431
  (73 shorter events, 50.5 us)
Async XLA Ops:
  0.7 4.6 copy-start
  68.5 231.6 %all-to-all-start = ((f32[2,8,512,320]{3,1,0,2:T(8,128)}), f32[2,8,512,320]{3,1,0,2:T(8,128)}, u32[]{:S(2)}, u32[]{:S(2)}) async-start(f32[2,8,512,320]{3,1,0,2:T(8,128)} %copy.13), calls=%async_computation | async-start | bytes 25165824 | tf_op jit(solution)/shard_map/all_to_all | solution.py:471
  340.5 146.3 %all-to-all-start.1 = ((f32[2,6,32,64,128]{4,3,2,1,0:T(8,128)}), f32[2,6,32,64,128]{4,3,2,1,0:T(8,128)}, u32[]{:S(2)}, u32[]{:S(2)}) async-start(f32[2,6,32,64,128]{4,3,2,1,0:T(8,128)} %shard_map.41), calls=%async_computation.1 | async-start | bytes 25165824 | tf_op jit(solution)/shard_map/all_to_all | solution.py:477
  504.2 69.9 %all-to-all-start.2 = ((f32[2,2,32,64,128]{4,3,2,1,0:T(8,128)}), f32[2,2,32,64,128]{4,3,2,1,0:T(8,128)}, u32[]{:S(2)}, u32[]{:S(2)}) async-start(f32[2,2,32,64,128]{4,3,2,1,0:T(8,128)} %pad_maximum_fusion.3), calls=%async_computation.2 | async-start | bytes 8388608 | tf_op jit(solution)/shard_map/all_to_all | solution.py:488
  510.9 23.3 %collective-permute-start.1 = (f32[3,4,64,128]{3,2,1,0:T(8,128)S(1)}, f32[3,4,64,128]{3,2,1,0:T(8,128)S(1)}, u32[]{:S(2)}, u32[]{:S(2)}) collective-permute-start(f32[3,4,64,128]{3,2,1,0:T(8,128)S(1)} %get-tuple-element.21), channel_id=1, source_target_pairs={{2,0},{4,2},{6,4},{8,6},{10,8},{12,10},{14,12},{16,14},{18,16},{20... | collective-permute-start | bytes 1179656 | tf_op jit(solution)/shard_map/ppermute | solution.py:26
  511.4 51.7 %collective-permute-start = (f32[3,4,64,128]{3,2,1,0:T(8,128)S(1)}, f32[3,4,64,128]{3,2,1,0:T(8,128)S(1)}, u32[]{:S(2)}, u32[]{:S(2)}) collective-permute-start(f32[3,4,64,128]{3,2,1,0:T(8,128)S(1)} %get-tuple-element.20), channel_id=1, source_target_pairs={{0,2},{2,4},{4,6},{6,8},{8,10},{10,12},{12,14},{14,16},{16,18},{18... | collective-permute-start | bytes 1179656 | tf_op jit(solution)/shard_map/ppermute | solution.py:23
  563.2 5.4 collective-permute-start.3
  564.7 6.5 collective-permute-start.2
  588.0 371.0 %all-to-all-start.3 = ((f32[16,32,2,8,128]{4,3,2,1,0:T(8,128)}), f32[16,32,2,8,128]{4,3,2,1,0:T(8,128)}, u32[]{:S(2)}, u32[]{:S(2)}) async-start(f32[16,32,2,8,128]{4,3,2,1,0:T(8,128)} %shard_map.42), calls=%async_computation.3 | async-start | bytes 8388608 | tf_op jit(solution)/shard_map/all_to_all | solution.py:76
  638.8 35.7 %collective-permute-start.4 = (f32[6,128,256]{2,1,0:T(8,128)S(1)}, f32[6,128,256]{2,1,0:T(8,128)S(1)}, u32[]{:S(2)}, u32[]{:S(2)}) collective-permute-start(f32[6,128,256]{2,1,0:T(8,128)S(1)} %get-tuple-element.17), channel_id=1, source_target_pairs={{0,2},{2,4},{4,6},{6,8},{8,10},{10,12},{12,14},{14,16},{16,18},{18... | collective-permute-start | bytes 2359304 | tf_op jit(solution)/shard_map/ppermute | solution.py:23
  640.5 39.0 %collective-permute-start.5 = (f32[6,128,256]{2,1,0:T(8,128)S(1)}, f32[6,128,256]{2,1,0:T(8,128)S(1)}, u32[]{:S(2)}, u32[]{:S(2)}) collective-permute-start(f32[6,128,256]{2,1,0:T(8,128)S(1)} %get-tuple-element.16), channel_id=1, source_target_pairs={{2,0},{4,2},{6,4},{8,6},{10,8},{12,10},{14,12},{16,14},{18,16},{20... | collective-permute-start | bytes 2359304 | tf_op jit(solution)/shard_map/ppermute | solution.py:26
  679.6 3.7 copy-start.1
  683.4 9.2 collective-permute-start.7
  683.5 15.7 %collective-permute-start.6 = (f32[76,8,256]{2,1,0:T(8,128)S(1)}, f32[76,8,256]{2,1,0:T(8,128)S(1)}, u32[]{:S(2)}, u32[]{:S(2)}) collective-permute-start(f32[76,8,256]{2,1,0:T(8,128)S(1)} %get-tuple-element.14), channel_id=1, source_target_pairs={{0,1},{1,0},{2,3},{3,2},{4,5},{5,4},{6,7},{7,6},{8,9},{9,8},{10,11... | collective-permute-start | bytes 1867784 | tf_op jit(solution)/shard_map/ppermute | solution.py:23
  993.3 112.1 %all-to-all-start.5 = ((f32[16,32,1,8,128]{4,3,2,1,0:T(8,128)}), f32[16,32,1,8,128]{4,3,2,1,0:T(8,128)S(1)}, u32[]{:S(2)}, u32[]{:S(2)}) async-start(f32[16,32,1,8,128]{4,3,2,1,0:T(8,128)} %shard_map.44), calls=%async_computation.5 | async-start | bytes 4194304 | tf_op jit(solution)/shard_map/all_to_all | solution.py:76
  1105.4 1.4 copy-start.2
